TPU v7x, 512 devices: a whole 4x4x16 slice. The times are simulated.
512 devices in a mesh: wave: 16 (over z_hi, y, core), tm: 32 (over z_lo, x).
Axes of the slice: x: 4, y: 4, z: 16 (z_hi: 2, z_lo: 8; z = z_hi * 8 + z_lo), core: 2. Of those that a mesh axis runs over, the one named last changes fastest.
Arguments:
- field: float32 [4, 128, 2, 2, 32768], P(None, 'wave', None, None, 'tm'), may hold values from -3 to 3
- lit_count: int32 [4], replicated, may hold values from 32 to 128
- route_fibre: int32 [4, 64], replicated, may hold values from 0 to 3, as said below
- route_slot: int32 [4, 64], replicated, may hold values from 0 to 63, as said below
- dispersion: float32 [2, 4], replicated, may hold values from 20 to 42
- nonlinearity: float32 [2, 4], replicated, may hold values from 0.25 to 2.5
Outputs:
- received: float32 [4, 128, 2, 2, 32768], P(None, 'wave', None, None, 'tm')
Inputs may be any that keep to these rules, and one draw needn't show every extreme that they name: `route_fibre`: together with route_slot it names every block of every fibre exactly once. `route_slot`: blocks 4 g .. 4 g + 3 of all fibres form channel group g. Of the 16 blocks of one group, at most 2 land in any one group, and every draw has pairs of groups with exactly 2.
All inputs are finite; a program needn't handle non-finite values.
Results may differ from a plain program's by a relative error of at most 0.0003.
Values sent between devices are 32-bit elements; how exact they have to be, the bound alone decides.
A program may use at most 64 MiB of HBM per device.

v0:
```python
import functools
import math

import jax
import jax.numpy as jnp
import numpy as np
from jax import lax
from jax.experimental import pallas as pl
from jax.experimental.pallas import tpu as pltpu
from jax.sharding import PartitionSpec as P

CH = 128
FIB = 4
LOC = 8
SEQ = 64
WAVE = 16
TM = 32
MESH = pl.DeviceIdType.MESH
F32 = jnp.float32
BF16 = jnp.bfloat16


def split_table(table):
    high = table.astype(jnp.bfloat16)
    low = (table - high.astype(np.float64)).astype(jnp.bfloat16)
    return high, low


def tables():
    eye = np.eye(8)
    r16 = np.arange(16)
    angle = 2.0 * np.pi * np.outer(r16, r16) / 16.0
    cos_a, sin_a = np.cos(angle), np.sin(angle)
    fwd = np.zeros((2, 16, 16, 2))
    fwd[0, :, :, 0], fwd[0, :, :, 1] = cos_a, sin_a
    fwd[1, :, :, 0], fwd[1, :, :, 1] = -sin_a, cos_a
    row_fwd = np.einsum("xrap,st->xsrtap", fwd, eye).reshape(256, 256)
    keep = np.zeros((8, 2, 2, 16))
    kc, ks = cos_a[4:12] / 2048.0, sin_a[4:12] / 2048.0
    keep[:, 0, 0], keep[:, 0, 1] = kc, -ks
    keep[:, 1, 0], keep[:, 1, 1] = ks, kc
    row_inv = np.einsum("apxr,st->sapxtr", keep, eye).reshape(128, 256)
    b = np.arange(128)
    angle = 2.0 * np.pi * (np.outer(b, b) % 128) / 128.0
    cos_b, sin_b = np.cos(angle), np.sin(angle)
    col_fwd = np.block([[cos_b, -sin_b], [sin_b, cos_b]])
    col_inv = np.block([[cos_b, sin_b], [-sin_b, cos_b]])
    twist = 2.0 * np.pi * np.outer(r16, b) / 2048.0
    out = []
    for table in (row_fwd, col_fwd, col_inv, row_inv):
        out.extend(split_table(table))
    out.append(np.cos(twist).astype(np.float32))
    out.append(np.sin(twist).astype(np.float32))
    return out


def fit(function, terms):
    nodes = np.cos(np.pi * (np.arange(400) + 0.5) / 400) * (np.pi * 1.02)
    square = nodes * nodes
    basis = np.stack([square**k for k in range(terms)], axis=1)
    return [float(v) for v in np.linalg.lstsq(basis, function(nodes), rcond=None)[0]]


SIN_POLY = fit(lambda x: np.sinc(x / np.pi), 8)
COS_POLY = fit(np.cos, 8)
TWO_PI = 2.0 * math.pi
PI_A = float(np.float32(6.28125))
PI_B = float(np.float32(np.round((TWO_PI - PI_A) * 2.0**24) / 2.0**24))
PI_B = float(np.floor((TWO_PI - PI_A) * 2.0**20) / 2.0**20)
PI_C = float(TWO_PI - PI_A - PI_B)


def sin_cos(angle):
    turns = jnp.floor(angle * (1.0 / TWO_PI) + 0.5)
    rest = ((angle - turns * PI_A) - turns * PI_B) - turns * PI_C
    square = rest * rest
    sine = jnp.full_like(square, SIN_POLY[-1])
    for value in SIN_POLY[-2::-1]:
        sine = sine * square + value
    cosine = jnp.full_like(square, COS_POLY[-1])
    for value in COS_POLY[-2::-1]:
        cosine = cosine * square + value
    return sine * rest, cosine


def split(x):
    high = x.astype(BF16)
    low = (x - high.astype(F32)).astype(BF16)
    return high, low


def dot(a, b):
    return jnp.dot(a, b, preferred_element_type=F32)


def left_product(table, data):
    high, low = split(data)
    return dot(table[0][...], high) + (dot(table[1][...], high) + dot(table[0][...], low))


def right_product(data, table):
    high, low = split(data)
    return dot(high, table[0][...]) + (dot(low, table[0][...]) + dot(high, table[1][...]))


def tiles(x):
    return x.reshape(-1, 8, 128)


def even_rows(shape):
    return lax.rem(lax.broadcasted_iota(jnp.int32, shape, len(shape) - 2), 2) == 0


def swap(x):
    t = tiles(x)
    even = even_rows(t.shape)
    return jnp.where(even, pltpu.roll(t, 7, 1), pltpu.roll(t, 1, 1)).reshape(x.shape)


def unpack_pair(x):
    t = tiles(x)
    even = even_rows(t.shape)
    first = jnp.where(even, t, pltpu.roll(t, 1, 1)).reshape(x.shape)
    second = jnp.where(even, pltpu.roll(t, 7, 1), t).reshape(x.shape)
    return first, second


def rotate(u, total, gain):
    square = u * u
    both = square[:, 0] + square[:, 1]
    power = both + swap(both)
    phase = gain * (2.0 * total[None] - power)
    sine, cosine = sin_cos(phase)
    signed = jnp.where(even_rows(sine.shape), -sine, sine)
    return u * cosine[:, None] + swap(u) * signed[:, None]


def disperse(u, t, filt_cos, filt_sin):
    rows = u.reshape(512, 128)
    x = jnp.concatenate([rows[:256], rows[256:]], axis=1)
    y = left_product(t["row_fwd"], x)
    tc = jnp.broadcast_to(t["twist_cos"][...][None], (8, 16, 128)).reshape(128, 128)
    ts = jnp.broadcast_to(t["twist_sin"][...][None], (8, 16, 128)).reshape(128, 128)
    halves = []
    for h in range(2):
        re = y[:128, h * 128 : (h + 1) * 128]
        im = y[128:, h * 128 : (h + 1) * 128]
        halves.append(jnp.concatenate([re * tc + im * ts, im * tc - re * ts], axis=1))
    spectrum = right_product(jnp.concatenate(halves, axis=0), t["col_fwd"])
    sr, si = spectrum[:, :128], spectrum[:, 128:]
    fc = jnp.broadcast_to(filt_cos[:, None], (8, 2, 16, 128)).reshape(256, 128)
    fs = jnp.broadcast_to(filt_sin[:, None], (8, 2, 16, 128)).reshape(256, 128)
    shaped = jnp.concatenate([sr * fc - si * fs, sr * fs + si * fc], axis=1)
    back = right_product(shaped, t["col_inv"])
    br, bi = back[:, :128], back[:, 128:]
    parts = []
    for h in range(2):
        re, im = br[h * 128 : (h + 1) * 128], bi[h * 128 : (h + 1) * 128]
        parts.append(jnp.concatenate([re * tc - im * ts, re * ts + im * tc], axis=0))
    out = left_product(t["row_inv"], jnp.concatenate(parts, axis=1))
    return jnp.concatenate([out[:, :128], out[:, 128:]], axis=0).reshape(16, 16, 128)


def kernel(
    lit, disp, nonlin, slot_item, take, take_fibre, field,
    rfh, rfl, cfh, cfl, cih, cil, rih, ril, twc, tws,
    out,
    filt_c, filt_s, halo, own, psum, pack, near, far, half_sum, total, q_side, q_ext,
    send_items, recv_items,
    halo_ss, halo_rs, near_ss, near_rs, far_ss, far_rs, side_ss, side_rs, item_ss, item_rs,
):
    t = dict(
        row_fwd=(rfh, rfl), col_fwd=(cfh, cfl), col_inv=(cih, cil), row_inv=(rih, ril),
        twist_cos=twc, twist_sin=tws,
    )
    me = lax.axis_index("wave")
    at = lax.axis_index("tm")
    my_z = me // 8
    my_y = lax.rem(me // 2, 4)
    my_core = lax.rem(me, 2)
    right = lax.rem(at + 1, TM)
    left = lax.rem(at + TM - 1, TM)

    def mate(k):
        kz, ky, kc = k // 8, (k // 2) % 4, k % 2
        return lax.rem(my_z + kz, 2) * 8 + lax.rem(my_y + ky, 4) * 2 + lax.rem(my_core + kc, 2)

    q_right = (lax.rem(me + 8 * (at // (TM - 1)), WAVE), right)
    q_left = (lax.rem(me + 8 * ((TM - 1 - at) // (TM - 1)), WAVE), left)
    d_right, d_left = (me, right), (me, left)

    barrier = pltpu.get_barrier_semaphore()
    for k in range(1, 16):
        pl.semaphore_signal(barrier, inc=1, device_id=(mate(k), at), device_id_type=MESH)
    for target in (d_right, d_left, q_right, q_left):
        pl.semaphore_signal(barrier, inc=1, device_id=target, device_id_type=MESH)

    r_i = lax.broadcasted_iota(jnp.int32, (16, 128), 0)
    m_i = lax.broadcasted_iota(jnp.int32, (16, 128), 1)
    k_i = r_i + 16 * m_i
    omega = jnp.where(k_i < 1024, k_i, k_i - 2048).astype(F32) * (2.0 * math.pi / 2048.0)

    def fill(i, carry):
        channel = (me * LOC + lax.rem(i, LOC)).astype(F32)
        offset = (math.pi / 2.0) * (2.0 * channel + 1.0 - CH) / CH
        for span in range(2):
            theta = disp[span, i // LOC] * (omega * omega + 2.0 * omega * offset)
            sine, cosine = sin_cos(theta)
            filt_s[span, i] = sine
            filt_c[span, i] = cosine
        return carry

    lax.fori_loop(0, FIB * LOC, fill, 0)
    pl.semaphore_wait(barrier, 19)

    def halo_copy(e, side, f, src):
        rows = pl.ds(8, 8) if side == 0 else pl.ds(0, 8)
        return pltpu.make_async_remote_copy(
            src_ref=src.at[pl.ds(f * 16, 16), rows],
            dst_ref=halo.at[e, side, pl.ds(f * 16, 16)],
            send_sem=halo_ss.at[e, side, f],
            recv_sem=halo_rs.at[e, side, f],
            device_id=d_right if side == 0 else d_left,
            device_id_type=MESH,
        )

    def own_of(e):
        return field if e == 0 else own.at[e - 1]

    def near_copy(e, k):
        return pltpu.make_async_remote_copy(
            src_ref=pack.at[e], dst_ref=near.at[e, k], send_sem=near_ss.at[e, k],
            recv_sem=near_rs.at[e, k], device_id=(mate(k), at), device_id_type=MESH,
        )

    def far_copy(e):
        return pltpu.make_async_remote_copy(
            src_ref=half_sum.at[e], dst_ref=far.at[e], send_sem=far_ss.at[e],
            recv_sem=far_rs.at[e], device_id=(mate(8), at), device_id_type=MESH,
        )

    def side_copy(e, side):
        rows = pl.ds(8, 8) if side == 0 else pl.ds(0, 8)
        return pltpu.make_async_remote_copy(
            src_ref=total.at[e, :, rows], dst_ref=q_side.at[e, side], send_sem=side_ss.at[e, side],
            recv_sem=side_rs.at[e, side], device_id=q_right if side == 0 else q_left,
            device_id_type=MESH,
        )

    def item_copy(k):
        return pltpu.make_async_remote_copy(
            src_ref=send_items.at[pl.ds(2 * k, 2)], dst_ref=recv_items.at[pl.ds(2 * k, 2)],
            send_sem=item_ss.at[k], recv_sem=item_rs.at[k], device_id=(mate(k), at),
            device_id_type=MESH,
        )

    def run_step(e, send_halo):
        span = e // 2
        source = own_of(e)

        def body(f, carry):
            halo_copy(e, 0, f, source).wait_recv()
            halo_copy(e, 1, f, source).wait_recv()
            group = pl.ds(f * 16, 16)
            u = jnp.concatenate([halo[e, 0, group], source[group], halo[e, 1, group]], axis=1)
            if e == 0:
                channel = me * LOC + lax.broadcasted_iota(jnp.int32, u.shape, 0) // 2
                u = jnp.where(channel < lit[f], u, 0.0)
            if e in (1, 3):
                u = rotate(
                    u.reshape(8, 2, 32, 128), q_ext[f], nonlin[span, f] * (1.0 / CH)
                ).reshape(16, 32, 128)
            table = pl.ds(f * LOC, LOC)
            result = disperse(u, t, filt_c[span, table], filt_s[span, table])
            own[e, group] = result
            if send_halo:
                halo_copy(e + 1, 0, f, own.at[e]).start()
                halo_copy(e + 1, 1, f, own.at[e]).start()
            both = jnp.sum(result * result, axis=0)
            psum[f] = both + swap(both)
            return carry

        lax.fori_loop(0, FIB, body, 0)
        even = even_rows((16, 128))
        for j in range(2):
            pack[e, j] = jnp.where(even, psum[2 * j], psum[2 * j + 1])
        for k in range(1, 8):
            near_copy(e, k).start()

    def finish_near(e):
        acc = pack[e]
        for k in range(1, 8):
            near_copy(e, k).wait_recv()
            acc = acc + near[e, k]
        half_sum[e] = acc
        far_copy(e).start()

    def finish_far(e, sides):
        far_copy(e).wait_recv()
        total[e] = half_sum[e] + far[e]
        if sides:
            side_copy(e, 0).start()
            side_copy(e, 1).start()
        for j in range(2):
            first, second = unpack_pair(total[e, j])
            q_ext[2 * j, 8:24] = first
            q_ext[2 * j + 1, 8:24] = second
        if sides:
            for side, rows in ((0, pl.ds(0, 8)), (1, pl.ds(24, 8))):
                side_copy(e, side).wait_recv()
                for j in range(2):
                    first, second = unpack_pair(q_side[e, side, j])
                    q_ext[2 * j, rows] = first
                    q_ext[2 * j + 1, rows] = second

    def start_halo(e, f, carry):
        halo_copy(e, 0, f, own_of(e)).start()
        halo_copy(e, 1, f, own_of(e)).start()
        return carry

    lax.fori_loop(0, FIB, functools.partial(start_halo, 0), 0)
    run_step(0, True)
    finish_near(0)
    finish_far(0, True)
    run_step(1, False)

    def gather(s, carry):
        send_items[s] = own[1, pl.ds(slot_item[s] * 4, 4)]
        return carry

    lax.fori_loop(0, 2 * WAVE, gather, 0)
    item_copy(8).start()
    finish_near(1)
    for k in (9, 10, 11, 12, 13, 14, 15, 1, 2, 3, 4, 5, 6, 7):
        item_copy(k).start()
    recv_items[0:2] = send_items[0:2]
    finish_far(1, False)
    for k in range(1, 16):
        item_copy(k).wait_recv()

    def place(i, carry):
        fibre = take_fibre[i]
        u = recv_items[take[i]].reshape(2, 2, 16, 128)
        u = rotate(u, q_ext[fibre, 8:24], nonlin[0, fibre] * (1.0 / CH))
        own[1, pl.ds(i * 4, 4)] = u.reshape(4, 16, 128)
        return carry

    def place_fibre(f, carry):
        lax.fori_loop(f * 4, f * 4 + 4, place, 0)
        return start_halo(2, f, carry)

    lax.fori_loop(0, FIB, place_fibre, 0)

    run_step(2, True)
    finish_near(2)
    finish_far(2, True)
    run_step(3, False)
    finish_near(3)
    finish_far(3, False)

    def last(f, carry):
        group = pl.ds(f * 16, 16)
        u = own[3, group].reshape(8, 2, 16, 128)
        u = rotate(u, q_ext[f, 8:24], nonlin[1, f] * (1.0 / CH))
        out[group] = u.reshape(16, 16, 128)
        return carry

    lax.fori_loop(0, FIB, last, 0)

    def drain_halo(f, carry):
        for e in range(4):
            halo_copy(e, 0, f, own_of(e)).wait_send()
            halo_copy(e, 1, f, own_of(e)).wait_send()
        return carry

    lax.fori_loop(0, FIB, drain_halo, 0)
    for e in range(4):
        for k in range(1, 8):
            near_copy(e, k).wait_send()
        far_copy(e).wait_send()
    for e in (0, 2):
        side_copy(e, 0).wait_send()
        side_copy(e, 1).wait_send()
    for k in range(1, 16):
        item_copy(k).wait_send()


def switch_tables(route_fibre, route_slot):
    me = lax.axis_index("wave")
    groups, blocks = WAVE, 4
    sends = FIB * blocks
    slot_all = route_slot.reshape(FIB, groups, blocks).transpose(1, 0, 2).reshape(groups, sends)
    fibre_all = route_fibre.reshape(FIB, groups, blocks).transpose(1, 0, 2).reshape(groups, sends)
    target_all = slot_all // blocks
    landing_all = fibre_all * blocks + slot_all % blocks
    position = jnp.arange(sends)
    earlier = (target_all[:, :, None] == target_all[:, None, :]) & (
        position[None, None, :] < position[None, :, None]
    )
    arrival_all = jnp.sum(earlier.astype(jnp.int32), axis=2)
    group = jnp.arange(groups)

    def offset(a, b):
        return (
            (a // 8 - b // 8) % 2 * 8
            + ((a // 2) % 4 - (b // 2) % 4) % 4 * 2
            + (a % 2 - b % 2) % 2
        )

    mine_from = (group == me)[:, None]
    my_target = jnp.sum(jnp.where(mine_from, target_all, 0), axis=0)
    my_arrival = jnp.sum(jnp.where(mine_from, arrival_all, 0), axis=0)
    slot_index = offset(my_target, me) * 2 + my_arrival
    matches = slot_index[None, :] == jnp.arange(2 * groups)[:, None]
    slot_item = jnp.sum(jnp.where(matches, position[None, :], 0), axis=1)
    receive = offset(me, group)[:, None] * 2 + arrival_all
    hits = (target_all == me)[:, :, None] & (landing_all[:, :, None] == position[None, None, :])
    take = jnp.sum(jnp.where(hits, receive[:, :, None], 0), axis=(0, 1))
    source_fibre = (position // blocks)[None, :, None]
    take_fibre = jnp.sum(jnp.where(hits, source_fibre, 0), axis=(0, 1))
    return slot_item.astype(jnp.int32), take.astype(jnp.int32), take_fibre.astype(jnp.int32)


def local(field, lit_count, route_fibre, route_slot, dispersion, nonlinearity):
    rows = field.reshape(FIB, LOC, 2, 2, 8, 128).transpose(0, 1, 2, 4, 3, 5).reshape(SEQ, 16, 128)
    slot_item, take, take_fibre = switch_tables(route_fibre, route_slot)
    constants = [jnp.asarray(v) for v in tables()]
    smem = pl.BlockSpec(memory_space=pltpu.SMEM)
    vmem = pl.BlockSpec(memory_space=pltpu.VMEM)
    dma = pltpu.SemaphoreType.DMA
    result = pl.pallas_call(
        kernel,
        out_shape=jax.ShapeDtypeStruct((SEQ, 16, 128), F32),
        in_specs=[smem] * 6 + [vmem] * 11,
        out_specs=vmem,
        scratch_shapes=[
            pltpu.VMEM((2, FIB * LOC, 16, 128), F32),
            pltpu.VMEM((2, FIB * LOC, 16, 128), F32),
            pltpu.VMEM((4, 2, SEQ, 8, 128), F32),
            pltpu.VMEM((4, SEQ, 16, 128), F32),
            pltpu.VMEM((FIB, 16, 128), F32),
            pltpu.VMEM((4, 2, 16, 128), F32),
            pltpu.VMEM((4, 8, 2, 16, 128), F32),
            pltpu.VMEM((4, 2, 16, 128), F32),
            pltpu.VMEM((4, 2, 16, 128), F32),
            pltpu.VMEM((4, 2, 16, 128), F32),
            pltpu.VMEM((4, 2, 2, 8, 128), F32),
            pltpu.VMEM((FIB, 32, 128), F32),
            pltpu.VMEM((2 * WAVE, 4, 16, 128), F32),
            pltpu.VMEM((2 * WAVE, 4, 16, 128), F32),
            dma((4, 2, FIB)), dma((4, 2, FIB)),
            dma((4, 8)), dma((4, 8)),
            dma((4,)), dma((4,)),
            dma((4, 2)), dma((4, 2)),
            dma((WAVE,)), dma((WAVE,)),
        ],
        compiler_params=pltpu.CompilerParams(
            collective_id=0, has_side_effects=True, vmem_limit_bytes=40 * 1024 * 1024
        ),
        name="propagate",
    )(lit_count, dispersion, nonlinearity, slot_item, take, take_fibre, rows, *constants)
    back = result.reshape(FIB, LOC, 2, 8, 2, 128).transpose(0, 1, 2, 4, 3, 5)
    return back.reshape(FIB, LOC, 2, 2, 1024)


def solution(mesh):
    return jax.shard_map(
        local,
        mesh=mesh,
        in_specs=(P(None, "wave", None, None, "tm"), P(), P(), P(), P(), P()),
        out_specs=P(None, "wave", None, None, "tm"),
        check_vma=False,
    )
```

profile of v0, /device:TPU:1, one launch (start us, length us, event | category | flops | bytes accessed | tf_op | source)
XLA Modules:
  0.0 157.6 jit_solution(6722156261727586737)
XLA Ops:
  0.1 0.7 broadcast_multiply_fusion
  0.8 0.1 mul.64
  0.9 0.1 copy.33
  1.0 0.1 copy.34
  1.1 0.8 reshape.369
  1.9 0.1 fusion.3
  2.0 0.1 reduce_sum.57
  2.1 0.1 copy.28
  2.2 0.1 copy.29
  2.3 0.4 convert_reduce_fusion
  2.7 0.1 broadcast_add_fusion
  2.8 0.2 select_reduce_fusion
  3.0 0.1 select_reduce_fusion.2.slot_item
  3.2 1.0 copy-done
  4.2 0.9 copy-done.4
  5.1 0.9 copy-done.5
  6.0 0.9 copy-done.6
  6.9 0.8 copy-done.8
  7.7 0.7 copy-done.10
  8.4 0.7 copy-done.11
  9.1 0.7 copy-done.12
  9.8 0.7 copy-done.13
  10.5 146.3 %propagate.1 = f32[64,16,128]{2,1,0:T(8,128)S(1)} custom-call(s32[4]{0:T(128)S(1)} %copy-done.13, f32[2,4]{1,0:T(2,128)S(1)} %copy-done.11, f32[2,4]{1,0:T(2,128)S(1)} %copy-done.12, s32[32]{0:T(128)S(1)} %select_reduce_fusion.2.slot_item, s32[16]{0:T(128)S(1)} %get-tuple-element.6.take, s32[16]{0:T(128)S(1)} %get-tuple-element.5.take_fibre, ...), custom_call_target="tpu_custom_call" | custom-call | tf_op jit(solution)/shard_map/propagate/pallas_call | solution.py:431
  156.8 0.8 copy.38
  (25 shorter events, 0.1 us)
Async XLA Ops:
  0.0 3.1 %copy-start.9 = (f32[16,128]{1,0:T(8,128)S(1)}, f32[16,128]{1,0:T(8,128)}, u32[]{:S(2)}) copy-start(f32[16,128]{1,0:T(8,128)} %constant.208.clone.tws) | copy-start | bytes 24580
  0.0 3.1 %copy-start.7 = (bf16[128,256]{1,0:T(8,128)(2,1)S(1)}, bf16[128,256]{1,0:T(8,128)(2,1)}, u32[]{:S(2)}) copy-start(bf16[128,256]{1,0:T(8,128)(2,1)} %constant.206.clone.ril) | copy-start | bytes 196612
  0.0 3.1 %copy-start.3 = (bf16[256,256]{1,0:T(8,128)(2,1)S(1)}, bf16[256,256]{1,0:T(8,128)(2,1)}, u32[]{:S(2)}) copy-start(bf16[256,256]{1,0:T(8,128)(2,1)} %constant.202.clone.cfl) | copy-start | bytes 393220
  1.1 2.1 %copy-start.1 = (bf16[256,256]{1,0:T(8,128)(2,1)S(1)}, bf16[256,256]{1,0:T(8,128)(2,1)}, u32[]{:S(2)}) copy-start(bf16[256,256]{1,0:T(8,128)(2,1)} %constant.204.clone.cil) | copy-start | bytes 393220
  1.1 2.1 %copy-start.2 = (bf16[256,256]{1,0:T(8,128)(2,1)S(1)}, bf16[256,256]{1,0:T(8,128)(2,1)}, u32[]{:S(2)}) copy-start(bf16[256,256]{1,0:T(8,128)(2,1)} %constant.203.clone.cih) | copy-start | bytes 393220
  3.1 1.0 copy-start
  4.2 0.9 copy-start.4
  5.1 0.9 copy-start.5
  6.0 0.9 copy-start.6
  6.9 0.8 copy-start.8
  7.7 0.7 copy-start.10
  8.4 0.7 copy-start.11
  9.1 0.7 copy-start.12
  9.8 0.7 copy-start.13
where the time goes:
time: 160 us; the launch traced here: 158 us
  Pallas kernels  146 us (91%)
  local copies, waits for them, and re-layouts  9.43 us (6%)
  other arithmetic  1.69 us (1%)
    pallas_call x1, Pallas kernels, local(): pl.pallas_call(kernel, out_shape=jax.ShapeDtypeStruct((SEQ, 16, 128), F32...  146 us
    unnamed x29, local copies, waits for them, and re-layouts  8.11 us

commit v1 on v0

v1 whole, which is shorter than its diff:
```python
import functools
import math

import jax
import jax.numpy as jnp
import numpy as np
from jax import lax
from jax.experimental import pallas as pl
from jax.experimental.pallas import tpu as pltpu
from jax.sharding import PartitionSpec as P

CH = 128
FIB = 4
LOC = 8
SEQ = 64
WAVE = 16
TM = 32
MESH = pl.DeviceIdType.MESH
F32 = jnp.float32
BF16 = jnp.bfloat16


def split_table(table):
    high = table.astype(jnp.bfloat16)
    low = (table - high.astype(np.float64)).astype(jnp.bfloat16)
    return high, low


def tables():
    eye = np.eye(8)
    r16 = np.arange(16)
    angle = 2.0 * np.pi * np.outer(r16, r16) / 16.0
    cos_a, sin_a = np.cos(angle), np.sin(angle)
    fwd = np.zeros((2, 16, 16, 2))
    fwd[0, :, :, 0], fwd[0, :, :, 1] = cos_a, sin_a
    fwd[1, :, :, 0], fwd[1, :, :, 1] = -sin_a, cos_a
    native = fwd.reshape(2, 16, 32)
    apart = np.concatenate(
        [
            fwd[:, :, lo:hi].transpose(0, 1, 3, 2).reshape(2, 16, -1)
            for lo, hi in ((0, 4), (4, 12), (12, 16))
        ],
        axis=2,
    )
    fwd_native, fwd_apart = (
        np.einsum("xrq,st->xsrtq", v, eye).reshape(256, 256) for v in (native, apart)
    )
    keep = np.zeros((8, 2, 2, 16))
    kc, ks = cos_a[4:12] / 2048.0, sin_a[4:12] / 2048.0
    keep[:, 0, 0], keep[:, 0, 1] = kc, -ks
    keep[:, 1, 0], keep[:, 1, 1] = ks, kc
    inv_native = np.einsum("apxr,st->sapxtr", keep, eye).reshape(128, 256)
    inv_apart = np.einsum("apxr,st->spaxtr", keep, eye).reshape(128, 256)
    b = np.arange(128)
    angle = 2.0 * np.pi * (np.outer(b, b) % 128) / 128.0
    cos_b, sin_b = np.cos(angle), np.sin(angle)
    col_fwd = np.block([[cos_b, -sin_b], [sin_b, cos_b]])
    col_inv = np.block([[cos_b, sin_b], [-sin_b, cos_b]])
    twist = 2.0 * np.pi * np.outer(r16, b) / 2048.0
    wide = []
    for table in (fwd_native, fwd_apart, col_fwd, col_inv):
        wide.extend(split_table(table))
    for table in (inv_native, inv_apart):
        wide.append(np.concatenate(split_table(table), axis=0))
    twist = np.stack([np.cos(twist), np.sin(twist)]).astype(np.float32)
    return jnp.asarray(np.stack(wide)), jnp.asarray(twist)


def fit(function, terms):
    nodes = np.cos(np.pi * (np.arange(400) + 0.5) / 400) * (np.pi * 1.02)
    square = nodes * nodes
    basis = np.stack([square**k for k in range(terms)], axis=1)
    return [float(v) for v in np.linalg.lstsq(basis, function(nodes), rcond=None)[0]]


SIN_POLY = fit(lambda x: np.sinc(x / np.pi), 7)
COS_POLY = fit(np.cos, 7)
TWO_PI = 2.0 * math.pi
PI_A = float(np.float32(6.28125))
PI_B = float(np.float32(np.round((TWO_PI - PI_A) * 2.0**24) / 2.0**24))
PI_B = float(np.floor((TWO_PI - PI_A) * 2.0**20) / 2.0**20)
PI_C = float(TWO_PI - PI_A - PI_B)


def sin_cos(angle):
    turns = jnp.floor(angle * (1.0 / TWO_PI) + 0.5)
    rest = ((angle - turns * PI_A) - turns * PI_B) - turns * PI_C
    square = rest * rest
    sine = jnp.full_like(square, SIN_POLY[-1])
    for value in SIN_POLY[-2::-1]:
        sine = sine * square + value
    cosine = jnp.full_like(square, COS_POLY[-1])
    for value in COS_POLY[-2::-1]:
        cosine = cosine * square + value
    return sine * rest, cosine


def split(x):
    high = x.astype(BF16)
    low = (x - high.astype(F32)).astype(BF16)
    return high, low


def dot(a, b):
    return jnp.dot(a, b, preferred_element_type=F32)


def left_product(table, data):
    high, low = split(data)
    return dot(table[0][...], high) + (dot(table[1][...], high) + dot(table[0][...], low))


def right_product(data, table):
    high, low = split(data)
    return dot(high, table[0][...]) + (dot(low, table[0][...]) + dot(high, table[1][...]))


def low_rows():
    return lax.broadcasted_iota(jnp.int32, (8, 128), 0) < 4


def even_rows():
    return lax.rem(lax.broadcasted_iota(jnp.int32, (8, 128), 0), 2) == 0


def turn(x, shift):
    return pltpu.roll(x.reshape(-1, 8, 128), shift, 1).reshape(x.shape)


def swap(x):
    t = x.reshape(-1, 8, 128)
    return jnp.where(even_rows()[None], pltpu.roll(t, 7, 1), pltpu.roll(t, 1, 1)).reshape(x.shape)


def unpack_pair(x):
    t = x.reshape(-1, 8, 128)
    even = even_rows()[None]
    first = jnp.where(even, t, pltpu.roll(t, 1, 1)).reshape(x.shape)
    second = jnp.where(even, pltpu.roll(t, 7, 1), t).reshape(x.shape)
    return first, second


def rotate_native(u, total, gain):
    square = u * u
    both = square[:, 0] + square[:, 1]
    phase = gain * (2.0 * total[None] - (both + swap(both)))
    sine, cosine = sin_cos(phase)
    t = sine.reshape(-1, 8, 128)
    signed = jnp.where(even_rows()[None], -t, t).reshape(sine.shape)
    return u * cosine[:, None] + swap(u) * signed[:, None]


def rotate_apart(u, total, gain):
    re, im = u[:, :, :8], u[:, :, 8:]
    square = re * re + im * im
    phase = gain * (2.0 * total[None] - (square[:, 0] + square[:, 1]))
    sine, cosine = sin_cos(phase)
    sine, cosine = sine[:, None], cosine[:, None]
    return jnp.concatenate([re * cosine - im * sine, re * sine + im * cosine], axis=2)


def rotate_edge(u, total, gain):
    square = u * u
    both = square[:, 0] + square[:, 1]
    phase = gain * (2.0 * total[None] - (both + turn(both, 4)))
    sine, cosine = sin_cos(phase)
    signed = jnp.where(low_rows()[None], -sine, sine)
    return u * cosine[:, None] + turn(u, 4) * signed[:, None]


def edges(u):
    re, im = u[..., :8, :], u[..., 8:, :]
    low = low_rows()
    return jnp.where(low, turn(re, 4), im), jnp.where(low, re, turn(im, 4))


def disperse(u, t, fwd, inv, filt_cos, filt_sin):
    rows = u.reshape(512, 128)
    x = jnp.concatenate([rows[:256], rows[256:]], axis=1)
    y = left_product(t[fwd], x)
    tc = jnp.broadcast_to(t["twist_cos"][...][None], (8, 16, 128)).reshape(128, 128)
    ts = jnp.broadcast_to(t["twist_sin"][...][None], (8, 16, 128)).reshape(128, 128)
    halves = []
    for h in range(2):
        re = y[:128, h * 128 : (h + 1) * 128]
        im = y[128:, h * 128 : (h + 1) * 128]
        halves.append(jnp.concatenate([re * tc + im * ts, im * tc - re * ts], axis=1))
    spectrum = right_product(jnp.concatenate(halves, axis=0), t["col_fwd"])
    sr, si = spectrum[:, :128], spectrum[:, 128:]
    fc = jnp.broadcast_to(filt_cos[:, None], (8, 2, 16, 128)).reshape(256, 128)
    fs = jnp.broadcast_to(filt_sin[:, None], (8, 2, 16, 128)).reshape(256, 128)
    shaped = jnp.concatenate([sr * fc - si * fs, sr * fs + si * fc], axis=1)
    back = right_product(shaped, t["col_inv"])
    br, bi = back[:, :128], back[:, 128:]
    parts = []
    for h in range(2):
        re, im = br[h * 128 : (h + 1) * 128], bi[h * 128 : (h + 1) * 128]
        parts.append(jnp.concatenate([re * tc - im * ts, re * ts + im * tc], axis=0))
    out = left_product(t[inv], jnp.concatenate(parts, axis=1))
    return jnp.concatenate([out[:, :128], out[:, 128:]], axis=0).reshape(16, 16, 128)


def kernel(
    lit, disp, nonlin, fibre_hbm, slot_hbm, field_hbm, wide_hbm, twist_hbm,
    out_hbm,
    wide, twist, route_f, route_s, launch, result_buf,
    filt_c, filt_s, halo, own, edge, pack, near, far, half_sum, total, q_side,
    send_items, recv_items, slot_item, take, take_fibre,
    load_s, out_s,
    halo_ss, halo_rs, near_ss, near_rs, far_ss, far_rs, side_ss, side_rs, item_ss, item_rs,
):
    t = dict(
        fwd_native=(wide.at[0], wide.at[1]), fwd_apart=(wide.at[2], wide.at[3]),
        col_fwd=(wide.at[4], wide.at[5]), col_inv=(wide.at[6], wide.at[7]),
        inv_native=(wide.at[8, pl.ds(0, 128)], wide.at[8, pl.ds(128, 128)]),
        inv_apart=(wide.at[9, pl.ds(0, 128)], wide.at[9, pl.ds(128, 128)]),
        twist_cos=twist.at[0], twist_sin=twist.at[1],
    )
    me = lax.axis_index("wave")
    at = lax.axis_index("tm")
    my_z = me // 8
    my_y = lax.rem(me // 2, 4)
    my_core = lax.rem(me, 2)
    right = lax.rem(at + 1, TM)
    left = lax.rem(at + TM - 1, TM)

    def mate(k):
        kz, ky, kc = k // 8, (k // 2) % 4, k % 2
        return lax.rem(my_z + kz, 2) * 8 + lax.rem(my_y + ky, 4) * 2 + lax.rem(my_core + kc, 2)

    q_right = (lax.rem(me + 8 * (at // (TM - 1)), WAVE), right)
    q_left = (lax.rem(me + 8 * ((TM - 1 - at) // (TM - 1)), WAVE), left)
    d_right, d_left = (me, right), (me, left)

    barrier = pltpu.get_barrier_semaphore()
    for k in range(1, 16):
        pl.semaphore_signal(barrier, inc=1, device_id=(mate(k), at), device_id_type=MESH)
    for target in (d_right, d_left, q_right, q_left):
        pl.semaphore_signal(barrier, inc=1, device_id=target, device_id_type=MESH)
    loads = [
        pltpu.make_async_copy(src, dst, load_s.at[i])
        for i, (src, dst) in enumerate(
            ((field_hbm, launch), (wide_hbm, wide), (twist_hbm, twist), (fibre_hbm, route_f), (slot_hbm, route_s))
        )
    ]
    for load in loads:
        load.start()

    r_i = lax.broadcasted_iota(jnp.int32, (16, 128), 0)
    m_i = lax.broadcasted_iota(jnp.int32, (16, 128), 1)
    k_i = r_i + 16 * m_i
    omega = jnp.where(k_i < 1024, k_i, k_i - 2048).astype(F32) * (2.0 * math.pi / 2048.0)

    def fill_tables(span):
        def fill(i, carry):
            channel = (me * LOC + lax.rem(i, LOC)).astype(F32)
            offset = (math.pi / 2.0) * (2.0 * channel + 1.0 - CH) / CH
            theta = disp[span, i // LOC] * (omega * omega + 2.0 * omega * offset)
            sine, cosine = sin_cos(theta)
            filt_s[span, i] = sine
            filt_c[span, i] = cosine
            return carry

        lax.fori_loop(0, FIB * LOC, fill, 0)

    def plan_switch():
        fibre_of = lax.broadcasted_iota(jnp.int32, (FIB, 64), 0)
        block_of = lax.broadcasted_iota(jnp.int32, (FIB, 64), 1)
        group_of = block_of // 4
        slot = route_s[...]
        target = slot // 4
        landing = route_f[...] * 4 + slot % 4
        key = landing * 16 + fibre_of * 4 + block_of % 4
        mine = group_of == me
        for k in range(16):
            here = mine & (target == mate(k))
            low = jnp.min(jnp.where(here, key, 4095))
            high = jnp.max(jnp.where(here, key, 0))
            slot_item[2 * k] = lax.rem(low, 16)
            slot_item[2 * k + 1] = lax.rem(high, 16)
        code = group_of * 4 + fibre_of
        groups = []
        for i in range(16):
            value = jnp.sum(jnp.where((target == me) & (landing == i), code, 0))
            group = lax.rem(value // 4, WAVE)
            before = jnp.int32(0)
            for other in groups:
                before = before + jnp.where(other == group, 1, 0)
            groups.append(group)
            kz = lax.rem(my_z - group // 8 + 2, 2)
            ky = lax.rem(my_y - lax.rem(group // 2, 4) + 4, 4)
            kc = lax.rem(my_core - lax.rem(group, 2) + 2, 2)
            take[i] = (kz * 8 + ky * 2 + kc) * 2 + jnp.minimum(before, 1)
            take_fibre[i] = lax.rem(value, 4)

    fill_tables(0)
    for load in loads:
        load.wait()
    pl.semaphore_wait(barrier, 19)

    def halo_copy(e, side, f):
        group = pl.ds(f * 16, 16)
        if e == 0:
            src = launch.at[group, pl.ds(8, 8) if side == 0 else pl.ds(0, 8)]
        else:
            src = edge.at[e - 1, side, group]
        return pltpu.make_async_remote_copy(
            src_ref=src,
            dst_ref=halo.at[e, side, group],
            send_sem=halo_ss.at[e, side, f],
            recv_sem=halo_rs.at[e, side, f],
            device_id=d_right if side == 0 else d_left,
            device_id_type=MESH,
        )

    def near_copy(e, k):
        return pltpu.make_async_remote_copy(
            src_ref=pack.at[e], dst_ref=near.at[e, k], send_sem=near_ss.at[e, k],
            recv_sem=near_rs.at[e, k], device_id=(mate(k), at), device_id_type=MESH,
        )

    def far_copy(e):
        return pltpu.make_async_remote_copy(
            src_ref=half_sum.at[e], dst_ref=far.at[e], send_sem=far_ss.at[e],
            recv_sem=far_rs.at[e], device_id=(mate(8), at), device_id_type=MESH,
        )

    def side_copy(e, side):
        return pltpu.make_async_remote_copy(
            src_ref=total.at[e], dst_ref=q_side.at[e, side], send_sem=side_ss.at[e, side],
            recv_sem=side_rs.at[e, side], device_id=q_right if side == 0 else q_left,
            device_id_type=MESH,
        )

    def item_copy(k):
        return pltpu.make_async_remote_copy(
            src_ref=send_items.at[pl.ds(2 * k, 2)], dst_ref=recv_items.at[pl.ds(2 * k, 2)],
            send_sem=item_ss.at[k], recv_sem=item_rs.at[k], device_id=(mate(k), at),
            device_id_type=MESH,
        )

    def keep_edges(e, f, u):
        group = pl.ds(f * 16, 16)
        edge[e, 0, group], edge[e, 1, group] = edges(u)
        halo_copy(e + 1, 0, f).start()
        halo_copy(e + 1, 1, f).start()

    def run_step(e, send_halo):
        span = e // 2

        def body(f, carry):
            halo_copy(e, 0, f).wait_recv()
            halo_copy(e, 1, f).wait_recv()
            group = pl.ds(f * 16, 16)
            parts = [halo[e, 0, group], launch[group] if e == 0 else own[e - 1, group], halo[e, 1, group]]
            if e in (1, 3):
                gain = nonlin[span, f] * (1.0 / CH)
                low = low_rows()
                before, after = q_side[e - 1, 0, f], q_side[e - 1, 1, f]
                sums = (
                    jnp.where(low, turn(before, 4), before),
                    total[e - 1, f],
                    jnp.where(low, after, turn(after, 4)),
                )
                turns = (rotate_edge, rotate_apart, rotate_edge)
                parts = [
                    rule(part.reshape(8, 2, *part.shape[1:]), q, gain).reshape(part.shape)
                    for rule, part, q in zip(turns, parts, sums)
                ]
            u = jnp.concatenate(parts, axis=1)
            if e == 0:
                channel = me * LOC + lax.broadcasted_iota(jnp.int32, (16, 1, 128), 0) // 2
                u = jnp.where(channel < lit[f], u, 0.0)
            table = pl.ds(f * LOC, LOC)
            result = disperse(
                u, t, "fwd_native" if e == 0 else "fwd_apart", "inv_native" if e == 3 else "inv_apart",
                filt_c[span, table], filt_s[span, table],
            )
            own[e, group] = result
            if send_halo:
                keep_edges(e, f, result)
            both = jnp.sum(result * result, axis=0)
            if e < 3:
                pack[e, f] = both[:8] + both[8:]
            else:
                full = both + swap(both)
                even = even_rows()
                row = f // 2 * 2
                for h in range(2):
                    part = full[h * 8 : h * 8 + 8]
                    old = pack[e, row + h]
                    pack[e, row + h] = jnp.where(even, jnp.where(lax.rem(f, 2) == 0, part, old), part)
            return carry

        lax.fori_loop(0, FIB, body, 0)
        for k in range(1, 8):
            near_copy(e, k).start()

    def finish_near(e):
        acc = pack[e]
        for k in range(1, 8):
            near_copy(e, k).wait_recv()
            acc = acc + near[e, k]
        half_sum[e] = acc
        far_copy(e).start()

    def finish_far(e, sides):
        far_copy(e).wait_recv()
        total[e] = half_sum[e] + far[e]
        if sides:
            side_copy(e, 0).start()
            side_copy(e, 1).start()
            side_copy(e, 0).wait_recv()
            side_copy(e, 1).wait_recv()

    def start_halo(f, carry):
        halo_copy(0, 0, f).start()
        halo_copy(0, 1, f).start()
        return carry

    lax.fori_loop(0, FIB, start_halo, 0)
    run_step(0, True)
    fill_tables(1)
    plan_switch()
    finish_near(0)
    finish_far(0, True)
    run_step(1, False)

    def gather(s, carry):
        send_items[s] = own[1, pl.ds(slot_item[s] * 4, 4)]
        return carry

    lax.fori_loop(0, 2 * WAVE, gather, 0)
    item_copy(8).start()
    finish_near(1)
    for k in (9, 10, 11, 12, 13, 14, 15, 1, 2, 3, 4, 5, 6, 7):
        item_copy(k).start()
    recv_items[0:2] = send_items[0:2]
    finish_far(1, False)
    for k in range(1, 16):
        item_copy(k).wait_recv()

    def place(i, carry):
        fibre = take_fibre[i]
        u = recv_items[take[i]].reshape(2, 2, 16, 128)
        u = rotate_apart(u, total[1, fibre], nonlin[0, fibre] * (1.0 / CH))
        own[1, pl.ds(i * 4, 4)] = u.reshape(4, 16, 128)
        return carry

    def place_fibre(f, carry):
        for i in range(4):
            place(f * 4 + i, carry)
        keep_edges(1, f, own[1, pl.ds(f * 16, 16)])
        return carry

    lax.fori_loop(0, FIB, place_fibre, 0)

    run_step(2, True)
    finish_near(2)
    finish_far(2, True)
    run_step(3, False)
    finish_near(3)
    finish_far(3, False)

    def store(f):
        group = pl.ds(f * 16, 16)
        return pltpu.make_async_copy(result_buf.at[group], out_hbm.at[group], out_s.at[f])

    def last(f, carry):
        group = pl.ds(f * 16, 16)
        u = own[3, group].reshape(8, 2, 16, 128)
        first, second = unpack_pair(total[3, pl.ds(f // 2 * 2, 2)].reshape(16, 128))
        q = jnp.where(lax.rem(f, 2) == 0, first, second)
        u = rotate_native(u, q, nonlin[1, f] * (1.0 / CH))
        result_buf[group] = u.reshape(16, 16, 128)
        store(f).start()
        return carry

    lax.fori_loop(0, FIB, last, 0)

    def drain_halo(f, carry):
        for e in range(4):
            halo_copy(e, 0, f).wait_send()
            halo_copy(e, 1, f).wait_send()
        return carry

    lax.fori_loop(0, FIB, drain_halo, 0)
    for e in range(4):
        for k in range(1, 8):
            near_copy(e, k).wait_send()
        far_copy(e).wait_send()
    for e in (0, 2):
        side_copy(e, 0).wait_send()
        side_copy(e, 1).wait_send()
    for k in range(1, 16):
        item_copy(k).wait_send()
    for f in range(FIB):
        store(f).wait()


def local(field, lit_count, route_fibre, route_slot, dispersion, nonlinearity):
    rows = field.reshape(FIB, LOC, 2, 2, 8, 128).transpose(0, 1, 2, 4, 3, 5).reshape(SEQ, 16, 128)
    wide, twist = tables()
    smem = pl.BlockSpec(memory_space=pltpu.SMEM)
    hbm = pl.BlockSpec(memory_space=pltpu.HBM)
    dma = pltpu.SemaphoreType.DMA
    result = pl.pallas_call(
        kernel,
        out_shape=jax.ShapeDtypeStruct((SEQ, 16, 128), F32),
        in_specs=[smem] * 3 + [hbm] * 5,
        out_specs=hbm,
        scratch_shapes=[
            pltpu.VMEM((10, 256, 256), BF16),
            pltpu.VMEM((2, 16, 128), F32),
            pltpu.VMEM((FIB, 64), jnp.int32),
            pltpu.VMEM((FIB, 64), jnp.int32),
            pltpu.VMEM((SEQ, 16, 128), F32),
            pltpu.VMEM((SEQ, 16, 128), F32),
            pltpu.VMEM((2, FIB * LOC, 16, 128), F32),
            pltpu.VMEM((2, FIB * LOC, 16, 128), F32),
            pltpu.VMEM((4, 2, SEQ, 8, 128), F32),
            pltpu.VMEM((4, SEQ, 16, 128), F32),
            pltpu.VMEM((3, 2, SEQ, 8, 128), F32),
            pltpu.VMEM((4, FIB, 8, 128), F32),
            pltpu.VMEM((4, 8, FIB, 8, 128), F32),
            pltpu.VMEM((4, FIB, 8, 128), F32),
            pltpu.VMEM((4, FIB, 8, 128), F32),
            pltpu.VMEM((4, FIB, 8, 128), F32),
            pltpu.VMEM((4, 2, FIB, 8, 128), F32),
            pltpu.VMEM((2 * WAVE, 4, 16, 128), F32),
            pltpu.VMEM((2 * WAVE, 4, 16, 128), F32),
            pltpu.SMEM((2 * WAVE,), jnp.int32),
            pltpu.SMEM((WAVE,), jnp.int32),
            pltpu.SMEM((WAVE,), jnp.int32),
            dma((5,)), dma((FIB,)),
            dma((4, 2, FIB)), dma((4, 2, FIB)),
            dma((4, 8)), dma((4, 8)),
            dma((4,)), dma((4,)),
            dma((4, 2)), dma((4, 2)),
            dma((WAVE,)), dma((WAVE,)),
        ],
        compiler_params=pltpu.CompilerParams(
            collective_id=0, has_side_effects=True, vmem_limit_bytes=67043328
        ),
        name="propagate",
    )(lit_count, dispersion, nonlinearity, route_fibre, route_slot, rows, wide, twist)
    back = result.reshape(FIB, LOC, 2, 8, 2, 128).transpose(0, 1, 2, 4, 3, 5)
    return back.reshape(FIB, LOC, 2, 2, 1024)


def solution(mesh):
    return jax.shard_map(
        local,
        mesh=mesh,
        in_specs=(P(None, "wave", None, None, "tm"), P(), P(), P(), P(), P()),
        out_specs=P(None, "wave", None, None, "tm"),
        check_vma=False,
    )
```

time: 160 us -> 149 us (0.931); the launches traced: 158 us -> 149 us
  local copies, waits for them, and re-layouts: 9.43 us -> 1.87 us
  other arithmetic: 1.69 us -> 0 us
    unnamed x29 -> x1, local copies, waits for them, and re-layouts: 8.11 us -> 1.87 us
where the time goes in v1:
time: 149 us
  Pallas kernels  147 us (99%)
  local copies, waits for them, and re-layouts  1.87 us (1%)
    pallas_call x1, Pallas kernels, local(): pl.pallas_call(kernel, out_shape=jax.ShapeDtypeStruct((SEQ, 16, 128), F32...  147 us

profile of v1, /device:TPU:1, one launch (start us, length us, event | category | flops | bytes accessed | tf_op | source)
XLA Modules:
  0.0 148.5 jit_solution(1064685689647670131)
XLA Ops:
  0.0 146.7 %propagate.1 = f32[64,16,128]{2,1,0:T(8,128)} custom-call(s32[4]{0:T(128)} %lit.1, f32[2,4]{1,0:T(2,128)} %disp.1, f32[2,4]{1,0:T(2,128)} %nonlin.1, s32[4,64]{1,0:T(4,128)} %fibre_hbm.1, s32[4,64]{1,0:T(4,128)} %slot_hbm.1, f32[64,16,128]{2,1,0:T(8,128)} %bitcast.11, bf16[10,256,256]{2,1,0:T(8,128)(2,1)} %constant.4.clone.wide_hbm, ...), custom_call_target="tpu_custom_call" | custom-call | tf_op jit(solution)/shard_map/propagate/pallas_call | solution.py:507
  146.7 1.9 %copy.12 = f32[4,8,2,2,1024]{4,3,2,1,0:T(2,128)} copy(f32[4,8,2,2,1024]{4,3,2,1,0:T(2,128)} %bitcast.10) | data formatting | bytes 1048576

commit v2 on v1

--- a/solution.py
+++ b/solution.py
@@ -10,6 +10,7 @@
 from jax.sharding import PartitionSpec as P
 
 CH = 128
+BLK = 2
 FIB = 4
 LOC = 8
 SEQ = 64
@@ -204,10 +205,12 @@
     lit, disp, nonlin, fibre_hbm, slot_hbm, field_hbm, wide_hbm, twist_hbm,
     out_hbm,
     wide, twist, route_f, route_s, launch, result_buf,
-    filt_c, filt_s, halo, own, edge, pack, near, far, half_sum, total, q_side,
-    send_items, recv_items, slot_item, take, take_fibre,
+    filt_c, filt_s, halo, own, edge, pack, near, far, half_sum, total, q_side0, q_side1, q_side2,
+    send_items, first_own, first_edge, first_halo, slot_own, slot_edge, slot_halo, slot_fc, slot_fs,
+    slot_item, slot_from, take, take_fibre,
     load_s, out_s,
     halo_ss, halo_rs, near_ss, near_rs, far_ss, far_rs, side_ss, side_rs, item_ss, item_rs,
+    first_ss, first_rs, group_ss, group_rs, second_ss, second_rs,
 ):
     t = dict(
         fwd_native=(wide.at[0], wide.at[1]), fwd_apart=(wide.at[2], wide.at[3]),
@@ -216,6 +219,7 @@
         inv_apart=(wide.at[9, pl.ds(0, 128)], wide.at[9, pl.ds(128, 128)]),
         twist_cos=twist.at[0], twist_sin=twist.at[1],
     )
+    q_side = (q_side0, q_side1, q_side2)
     me = lax.axis_index("wave")
     at = lax.axis_index("tm")
     my_z = me // 8
@@ -224,8 +228,10 @@
     right = lax.rem(at + 1, TM)
     left = lax.rem(at + TM - 1, TM)
 
-    def mate(k):
-        kz, ky, kc = k // 8, (k // 2) % 4, k % 2
+    def mate(k, sign=1):
+        kz, ky, kc = lax.div(k, 8), lax.rem(lax.div(k, 2), 4), lax.rem(k, 2)
+        if sign < 0:
+            ky = 4 - ky
         return lax.rem(my_z + kz, 2) * 8 + lax.rem(my_y + ky, 4) * 2 + lax.rem(my_core + kc, 2)
 
     q_right = (lax.rem(me + 8 * (at // (TM - 1)), WAVE), right)
@@ -276,8 +282,10 @@
             here = mine & (target == mate(k))
             low = jnp.min(jnp.where(here, key, 4095))
             high = jnp.max(jnp.where(here, key, 0))
-            slot_item[2 * k] = lax.rem(low, 16)
-            slot_item[2 * k + 1] = lax.rem(high, 16)
+            slot_item[k] = lax.rem(low, 16)
+            slot_item[16 + k] = lax.rem(high, 16)
+            here = (group_of == mate(k, -1)) & (target == me)
+            slot_from[k] = lax.rem(jnp.min(jnp.where(here, key, 4095)), 16)
         code = group_of * 4 + fibre_of
         groups = []
         for i in range(16):
@@ -290,12 +298,25 @@
             kz = lax.rem(my_z - group // 8 + 2, 2)
             ky = lax.rem(my_y - lax.rem(group // 2, 4) + 4, 4)
             kc = lax.rem(my_core - lax.rem(group, 2) + 2, 2)
-            take[i] = (kz * 8 + ky * 2 + kc) * 2 + jnp.minimum(before, 1)
+            take[i] = jnp.minimum(before, 1) * 16 + kz * 8 + ky * 2 + kc
             take_fibre[i] = lax.rem(value, 4)
+
+    def fill_slots(k, carry):
+        item = slot_from[k]
+        source = mate(k, -1)
+        for c in range(BLK):
+            channel = (source * LOC + lax.rem(item, 4) * BLK + c).astype(F32)
+            offset = (math.pi / 2.0) * (2.0 * channel + 1.0 - CH) / CH
+            theta = disp[0, lax.div(item, 4)] * (omega * omega + 2.0 * omega * offset)
+            sine, cosine = sin_cos(theta)
+            slot_fs[k * BLK + c] = sine
+            slot_fc[k * BLK + c] = cosine
+        return carry
 
     fill_tables(0)
     for load in loads:
         load.wait()
+    plan_switch()
     pl.semaphore_wait(barrier, 19)
 
     def halo_copy(e, side, f):
@@ -327,16 +348,40 @@
 
     def side_copy(e, side):
         return pltpu.make_async_remote_copy(
-            src_ref=total.at[e], dst_ref=q_side.at[e, side], send_sem=side_ss.at[e, side],
+            src_ref=total.at[e], dst_ref=q_side[e].at[side], send_sem=side_ss.at[e, side],
             recv_sem=side_rs.at[e, side], device_id=q_right if side == 0 else q_left,
             device_id_type=MESH,
         )
 
-    def item_copy(k):
+    def item_copy(j, k):
         return pltpu.make_async_remote_copy(
-            src_ref=send_items.at[pl.ds(2 * k, 2)], dst_ref=recv_items.at[pl.ds(2 * k, 2)],
-            send_sem=item_ss.at[k], recv_sem=item_rs.at[k], device_id=(mate(k), at),
+            src_ref=send_items.at[j, k], dst_ref=first_own.at[k] if j == 0 else slot_own.at[16 + k],
+            send_sem=item_ss.at[j, k], recv_sem=item_rs.at[j, k], device_id=(mate(k), at),
             device_id_type=MESH,
+        )
+
+    def to_side(src, dst, send_sem, recv_sem, side):
+        return pltpu.make_async_remote_copy(
+            src_ref=src, dst_ref=dst, send_sem=send_sem, recv_sem=recv_sem,
+            device_id=d_right if side == 0 else d_left, device_id_type=MESH,
+        )
+
+    def first_copy(side, k):
+        return to_side(
+            first_edge.at[side, k], first_halo.at[side, k], first_ss.at[side, k], first_rs.at[side, k], side
+        )
+
+    def group_copy(side, g):
+        slots = pl.ds(g * 4, 4)
+        return to_side(
+            slot_edge.at[side, slots], slot_halo.at[side, slots], group_ss.at[side, g],
+            group_rs.at[side, g], side,
+        )
+
+    def second_copy(side, k):
+        return to_side(
+            slot_edge.at[side, 16 + k], slot_halo.at[side, 16 + k], second_ss.at[side, k],
+            second_rs.at[side, k], side,
         )
 
     def keep_edges(e, f, u):
@@ -345,32 +390,47 @@
         halo_copy(e + 1, 0, f).start()
         halo_copy(e + 1, 1, f).start()
 
+    def turned(parts, channels, e, fibre, gain):
+        low = low_rows()
+        before, after = q_side[e][0, fibre], q_side[e][1, fibre]
+        sums = (
+            jnp.where(low, turn(before, 4), before),
+            total[e, fibre],
+            jnp.where(low, after, turn(after, 4)),
+        )
+        turns = (rotate_edge, rotate_apart, rotate_edge)
+        return jnp.concatenate(
+            [
+                rule(part.reshape(channels, 2, *part.shape[1:]), q, gain).reshape(part.shape)
+                for rule, part, q in zip(turns, parts, sums)
+            ],
+            axis=1,
+        )
+
+    def placed(f):
+        blocks = []
+        for i in range(4):
+            slot, fibre = take[f * 4 + i], take_fibre[f * 4 + i]
+            parts = [slot_halo[0, slot], slot_own[slot], slot_halo[1, slot]]
+            blocks.append(turned(parts, BLK, 1, fibre, nonlin[0, fibre] * (1.0 / CH)))
+        return jnp.concatenate(blocks, axis=0)
+
     def run_step(e, send_halo):
         span = e // 2
 
         def body(f, carry):
-            halo_copy(e, 0, f).wait_recv()
-            halo_copy(e, 1, f).wait_recv()
             group = pl.ds(f * 16, 16)
-            parts = [halo[e, 0, group], launch[group] if e == 0 else own[e - 1, group], halo[e, 1, group]]
-            if e in (1, 3):
-                gain = nonlin[span, f] * (1.0 / CH)
-                low = low_rows()
-                before, after = q_side[e - 1, 0, f], q_side[e - 1, 1, f]
-                sums = (
-                    jnp.where(low, turn(before, 4), before),
-                    total[e - 1, f],
-                    jnp.where(low, after, turn(after, 4)),
-                )
-                turns = (rotate_edge, rotate_apart, rotate_edge)
-                parts = [
-                    rule(part.reshape(8, 2, *part.shape[1:]), q, gain).reshape(part.shape)
-                    for rule, part, q in zip(turns, parts, sums)
-                ]
-            u = jnp.concatenate(parts, axis=1)
-            if e == 0:
-                channel = me * LOC + lax.broadcasted_iota(jnp.int32, (16, 1, 128), 0) // 2
-                u = jnp.where(channel < lit[f], u, 0.0)
+            if e == 2:
+                u = placed(f)
+            else:
+                halo_copy(e, 0, f).wait_recv()
+                halo_copy(e, 1, f).wait_recv()
+                parts = [halo[e, 0, group], launch[group] if e == 0 else own[e - 1, group], halo[e, 1, group]]
+                if e == 0:
+                    channel = me * LOC + lax.broadcasted_iota(jnp.int32, (16, 1, 128), 0) // 2
+                    u = jnp.where(channel < lit[f], jnp.concatenate(parts, axis=1), 0.0)
+                else:
+                    u = turned(parts, LOC, e - 1, f, nonlin[span, f] * (1.0 / CH))
             table = pl.ds(f * LOC, LOC)
             result = disperse(
                 u, t, "fwd_native" if e == 0 else "fwd_apart", "inv_native" if e == 3 else "inv_apart",
@@ -396,6 +456,46 @@
         for k in range(1, 8):
             near_copy(e, k).start()
 
+    def gather(j):
+        def one(k, carry):
+            send_items[j, k] = own[j, pl.ds(slot_item[16 * j + k] * 4, 4)]
+            return carry
+
+        lax.fori_loop(0, WAVE, one, 0)
+        (first_own if j == 0 else slot_own)[16 * j] = send_items[j, 0]
+
+    def forward_first(k):
+        first_edge[0, k], first_edge[1, k] = edges(first_own[k])
+        first_copy(0, k).start()
+        first_copy(1, k).start()
+
+    def forward_second(k):
+        slot_edge[0, 16 + k], slot_edge[1, 16 + k] = edges(slot_own[16 + k])
+        second_copy(0, k).start()
+        second_copy(1, k).start()
+
+    def first_slots(g, carry):
+        blocks = []
+        for i in range(4):
+            k = g * 4 + i
+            first_copy(0, k).wait_recv()
+            first_copy(1, k).wait_recv()
+            fibre = lax.div(slot_from[k], 4)
+            parts = [first_halo[0, k], first_own[k], first_halo[1, k]]
+            blocks.append(turned(parts, BLK, 0, fibre, nonlin[0, fibre] * (1.0 / CH)))
+        table = pl.ds(g * LOC, LOC)
+        result = disperse(
+            jnp.concatenate(blocks, axis=0), t, "fwd_apart", "inv_apart", slot_fc[table], slot_fs[table]
+        )
+        slots = pl.ds(g * 4, 4)
+        slot_own[slots] = result.reshape(4, 4, 16, 128)
+        up, down = edges(result)
+        slot_edge[0, slots] = up.reshape(4, 4, 8, 128)
+        slot_edge[1, slots] = down.reshape(4, 4, 8, 128)
+        group_copy(0, g).start()
+        group_copy(1, g).start()
+        return carry
+
     def finish_near(e):
         acc = pack[e]
         for k in range(1, 8):
@@ -419,41 +519,39 @@
         return carry
 
     lax.fori_loop(0, FIB, start_halo, 0)
+    fill_tables(1)
+    lax.fori_loop(0, WAVE, fill_slots, 0)
     run_step(0, True)
-    fill_tables(1)
-    plan_switch()
+    gather(0)
+    item_copy(0, 8).start()
     finish_near(0)
+    order = (9, 10, 11, 12, 13, 14, 15, 1, 2, 3, 4, 5, 6, 7)
+    for k in order:
+        item_copy(0, k).start()
     finish_far(0, True)
     run_step(1, False)
-
-    def gather(s, carry):
-        send_items[s] = own[1, pl.ds(slot_item[s] * 4, 4)]
-        return carry
-
-    lax.fori_loop(0, 2 * WAVE, gather, 0)
-    item_copy(8).start()
+    gather(1)
+    item_copy(1, 8).start()
     finish_near(1)
-    for k in (9, 10, 11, 12, 13, 14, 15, 1, 2, 3, 4, 5, 6, 7):
-        item_copy(k).start()
-    recv_items[0:2] = send_items[0:2]
-    finish_far(1, False)
-    for k in range(1, 16):
-        item_copy(k).wait_recv()
-
-    def place(i, carry):
-        fibre = take_fibre[i]
-        u = recv_items[take[i]].reshape(2, 2, 16, 128)
-        u = rotate_apart(u, total[1, fibre], nonlin[0, fibre] * (1.0 / CH))
-        own[1, pl.ds(i * 4, 4)] = u.reshape(4, 16, 128)
-        return carry
-
-    def place_fibre(f, carry):
-        for i in range(4):
-            place(f * 4 + i, carry)
-        keep_edges(1, f, own[1, pl.ds(f * 16, 16)])
-        return carry
-
-    lax.fori_loop(0, FIB, place_fibre, 0)
+    for k in order:
+        item_copy(1, k).start()
+
+    forward_first(0)
+    for k in (1, 2, 3, 4, 5, 6, 7, 8, 9, 10, 11, 12, 13, 14, 15):
+        item_copy(0, k).wait_recv()
+        forward_first(k)
+    forward_second(0)
+    lax.fori_loop(0, 4, first_slots, 0)
+    finish_far(1, True)
+    for k in (1, 2, 3, 4, 5, 6, 7, 8, 9, 10, 11, 12, 13, 14, 15):
+        item_copy(1, k).wait_recv()
+        forward_second(k)
+    for g in range(4):
+        group_copy(0, g).wait_recv()
+        group_copy(1, g).wait_recv()
+    for k in range(16):
+        second_copy(0, k).wait_recv()
+        second_copy(1, k).wait_recv()
 
     run_step(2, True)
     finish_near(2)
@@ -479,7 +577,7 @@
     lax.fori_loop(0, FIB, last, 0)
 
     def drain_halo(f, carry):
-        for e in range(4):
+        for e in (0, 1, 3):
             halo_copy(e, 0, f).wait_send()
             halo_copy(e, 1, f).wait_send()
         return carry
@@ -489,11 +587,18 @@
         for k in range(1, 8):
             near_copy(e, k).wait_send()
         far_copy(e).wait_send()
-    for e in (0, 2):
+    for e in range(3):
         side_copy(e, 0).wait_send()
         side_copy(e, 1).wait_send()
     for k in range(1, 16):
-        item_copy(k).wait_send()
+        item_copy(0, k).wait_send()
+        item_copy(1, k).wait_send()
+    for side in range(2):
+        for k in range(16):
+            first_copy(side, k).wait_send()
+            second_copy(side, k).wait_send()
+        for g in range(4):
+            group_copy(side, g).wait_send()
     for f in range(FIB):
         store(f).wait()
 
@@ -526,10 +631,20 @@
             pltpu.VMEM((4, FIB, 8, 128), F32),
             pltpu.VMEM((4, FIB, 8, 128), F32),
             pltpu.VMEM((4, FIB, 8, 128), F32),
-            pltpu.VMEM((4, 2, FIB, 8, 128), F32),
+            pltpu.VMEM((2, FIB, 8, 128), F32),
+            pltpu.VMEM((2, FIB, 8, 128), F32),
+            pltpu.VMEM((2, FIB, 8, 128), F32),
+            pltpu.VMEM((2, WAVE, 4, 16, 128), F32),
+            pltpu.VMEM((WAVE, 4, 16, 128), F32),
+            pltpu.VMEM((2, WAVE, 4, 8, 128), F32),
+            pltpu.VMEM((2, WAVE, 4, 8, 128), F32),
             pltpu.VMEM((2 * WAVE, 4, 16, 128), F32),
-            pltpu.VMEM((2 * WAVE, 4, 16, 128), F32),
+            pltpu.VMEM((2, 2 * WAVE, 4, 8, 128), F32),
+            pltpu.VMEM((2, 2 * WAVE, 4, 8, 128), F32),
+            pltpu.VMEM((2 * WAVE, 16, 128), F32),
+            pltpu.VMEM((2 * WAVE, 16, 128), F32),
             pltpu.SMEM((2 * WAVE,), jnp.int32),
+            pltpu.SMEM((WAVE,), jnp.int32),
             pltpu.SMEM((WAVE,), jnp.int32),
             pltpu.SMEM((WAVE,), jnp.int32),
             dma((5,)), dma((FIB,)),
@@ -537,7 +652,10 @@
             dma((4, 8)), dma((4, 8)),
             dma((4,)), dma((4,)),
             dma((4, 2)), dma((4, 2)),
-            dma((WAVE,)), dma((WAVE,)),
+            dma((2, WAVE)), dma((2, WAVE)),
+            dma((2, WAVE)), dma((2, WAVE)),
+            dma((2, FIB)), dma((2, FIB)),
+            dma((2, WAVE)), dma((2, WAVE)),
         ],
         compiler_params=pltpu.CompilerParams(
             collective_id=0, has_side_effects=True, vmem_limit_bytes=67043328

time: 149 us -> 157 us (1.054)
  Pallas kernels: 147 us -> 155 us
    pallas_call x1, Pallas kernels: 147 us -> 155 us  [local(): pl.pallas_call(kernel, out_shape=jax.ShapeDtypeStruct((SEQ, 16, 128), F32...]
where the time goes in v2:
time: 157 us
  Pallas kernels  155 us (99%)
  local copies, waits for them, and re-layouts  1.87 us (1%)
    pallas_call x1, Pallas kernels, local(): pl.pallas_call(kernel, out_shape=jax.ShapeDtypeStruct((SEQ, 16, 128), F32...  155 us

profile of v2, /device:TPU:1, one launch (start us, length us, event | category | flops | bytes accessed | tf_op | source)
XLA Modules:
  0.0 157.2 jit_solution(1257221139009083478)
XLA Ops:
  0.0 155.4 %propagate.1 = f32[64,16,128]{2,1,0:T(8,128)} custom-call(s32[4]{0:T(128)} %lit.1, f32[2,4]{1,0:T(2,128)} %disp.1, f32[2,4]{1,0:T(2,128)} %nonlin.1, s32[4,64]{1,0:T(4,128)} %fibre_hbm.1, s32[4,64]{1,0:T(4,128)} %slot_hbm.1, f32[64,16,128]{2,1,0:T(8,128)} %bitcast.11, bf16[10,256,256]{2,1,0:T(8,128)(2,1)} %constant.4.clone.wide_hbm, ...), custom_call_target="tpu_custom_call" | custom-call | tf_op jit(solution)/shard_map/propagate/pallas_call | solution.py:612
  155.4 1.9 %copy.12 = f32[4,8,2,2,1024]{4,3,2,1,0:T(2,128)} copy(f32[4,8,2,2,1024]{4,3,2,1,0:T(2,128)} %bitcast.10) | data formatting | bytes 1048576

commit v3 on v2

--- a/solution.py
+++ b/solution.py
@@ -205,12 +205,12 @@
     lit, disp, nonlin, fibre_hbm, slot_hbm, field_hbm, wide_hbm, twist_hbm,
     out_hbm,
     wide, twist, route_f, route_s, launch, result_buf,
-    filt_c, filt_s, halo, own, edge, pack, near, far, half_sum, total, q_side0, q_side1, q_side2,
-    send_items, first_own, first_edge, first_halo, slot_own, slot_edge, slot_halo, slot_fc, slot_fs,
+    filt_c, filt_s, halo, own, edge, pack, near, far, half_sum, total, q_side0, q_side2,
+    send_items, send_edge, first_own, first_edge, first_halo, slot_own, slot_fc, slot_fs,
     slot_item, slot_from, take, take_fibre,
     load_s, out_s,
     halo_ss, halo_rs, near_ss, near_rs, far_ss, far_rs, side_ss, side_rs, item_ss, item_rs,
-    first_ss, first_rs, group_ss, group_rs, second_ss, second_rs,
+    first_ss, first_rs,
 ):
     t = dict(
         fwd_native=(wide.at[0], wide.at[1]), fwd_apart=(wide.at[2], wide.at[3]),
@@ -219,7 +219,7 @@
         inv_apart=(wide.at[9, pl.ds(0, 128)], wide.at[9, pl.ds(128, 128)]),
         twist_cos=twist.at[0], twist_sin=twist.at[1],
     )
-    q_side = (q_side0, q_side1, q_side2)
+    q_side = {0: q_side0, 2: q_side2}
     me = lax.axis_index("wave")
     at = lax.axis_index("tm")
     my_z = me // 8
@@ -243,6 +243,15 @@
         pl.semaphore_signal(barrier, inc=1, device_id=(mate(k), at), device_id_type=MESH)
     for target in (d_right, d_left, q_right, q_left):
         pl.semaphore_signal(barrier, inc=1, device_id=target, device_id_type=MESH)
+    is_last = at // (TM - 1)
+    is_first = (TM - 1 - at) // (TM - 1)
+
+    @pl.when(is_last + is_first > 0)
+    def _():
+        across = lax.rem(at + is_last + TM - is_first, TM)
+        for k in range(8, 16):
+            pl.semaphore_signal(barrier, inc=1, device_id=(mate(k), across), device_id_type=MESH)
+
     loads = [
         pltpu.make_async_copy(src, dst, load_s.at[i])
         for i, (src, dst) in enumerate(
@@ -302,8 +311,8 @@
             take_fibre[i] = lax.rem(value, 4)
 
     def fill_slots(k, carry):
-        item = slot_from[k]
-        source = mate(k, -1)
+        item = slot_from[8 + k]
+        source = mate(8 + k, -1)
         for c in range(BLK):
             channel = (source * LOC + lax.rem(item, 4) * BLK + c).astype(F32)
             offset = (math.pi / 2.0) * (2.0 * channel + 1.0 - CH) / CH
@@ -317,7 +326,7 @@
     for load in loads:
         load.wait()
     plan_switch()
-    pl.semaphore_wait(barrier, 19)
+    pl.semaphore_wait(barrier, 19 + 8 * (is_last + is_first))
 
     def halo_copy(e, side, f):
         group = pl.ds(f * 16, 16)
@@ -354,34 +363,19 @@
         )
 
     def item_copy(j, k):
+        early = j == 0 and k >= 8
         return pltpu.make_async_remote_copy(
-            src_ref=send_items.at[j, k], dst_ref=first_own.at[k] if j == 0 else slot_own.at[16 + k],
+            src_ref=send_items.at[j, k], dst_ref=first_own.at[k - 8] if early else slot_own.at[16 * j + k],
             send_sem=item_ss.at[j, k], recv_sem=item_rs.at[j, k], device_id=(mate(k), at),
             device_id_type=MESH,
         )
 
-    def to_side(src, dst, send_sem, recv_sem, side):
+    def first_copy(side, k, straight=False):
+        target = right if side == 0 else left
         return pltpu.make_async_remote_copy(
-            src_ref=src, dst_ref=dst, send_sem=send_sem, recv_sem=recv_sem,
-            device_id=d_right if side == 0 else d_left, device_id_type=MESH,
-        )
-
-    def first_copy(side, k):
-        return to_side(
-            first_edge.at[side, k], first_halo.at[side, k], first_ss.at[side, k], first_rs.at[side, k], side
-        )
-
-    def group_copy(side, g):
-        slots = pl.ds(g * 4, 4)
-        return to_side(
-            slot_edge.at[side, slots], slot_halo.at[side, slots], group_ss.at[side, g],
-            group_rs.at[side, g], side,
-        )
-
-    def second_copy(side, k):
-        return to_side(
-            slot_edge.at[side, 16 + k], slot_halo.at[side, 16 + k], second_ss.at[side, k],
-            second_rs.at[side, k], side,
+            src_ref=(send_edge if straight else first_edge).at[side, k], dst_ref=first_halo.at[side, k],
+            send_sem=first_ss.at[side, k], recv_sem=first_rs.at[side, k],
+            device_id=(mate(8 + k) if straight else me, target), device_id_type=MESH,
         )
 
     def keep_edges(e, f, u):
@@ -407,30 +401,21 @@
             axis=1,
         )
 
-    def placed(f):
-        blocks = []
-        for i in range(4):
-            slot, fibre = take[f * 4 + i], take_fibre[f * 4 + i]
-            parts = [slot_halo[0, slot], slot_own[slot], slot_halo[1, slot]]
-            blocks.append(turned(parts, BLK, 1, fibre, nonlin[0, fibre] * (1.0 / CH)))
-        return jnp.concatenate(blocks, axis=0)
-
     def run_step(e, send_halo):
         span = e // 2
 
         def body(f, carry):
             group = pl.ds(f * 16, 16)
-            if e == 2:
-                u = placed(f)
+            halo_copy(e, 0, f).wait_recv()
+            halo_copy(e, 1, f).wait_recv()
+            parts = [halo[e, 0, group], launch[group] if e == 0 else own[e - 1, group], halo[e, 1, group]]
+            if e in (1, 3):
+                u = turned(parts, LOC, e - 1, f, nonlin[span, f] * (1.0 / CH))
             else:
-                halo_copy(e, 0, f).wait_recv()
-                halo_copy(e, 1, f).wait_recv()
-                parts = [halo[e, 0, group], launch[group] if e == 0 else own[e - 1, group], halo[e, 1, group]]
-                if e == 0:
-                    channel = me * LOC + lax.broadcasted_iota(jnp.int32, (16, 1, 128), 0) // 2
-                    u = jnp.where(channel < lit[f], jnp.concatenate(parts, axis=1), 0.0)
-                else:
-                    u = turned(parts, LOC, e - 1, f, nonlin[span, f] * (1.0 / CH))
+                u = jnp.concatenate(parts, axis=1)
+            if e == 0:
+                channel = me * LOC + lax.broadcasted_iota(jnp.int32, (16, 1, 128), 0) // 2
+                u = jnp.where(channel < lit[f], u, 0.0)
             table = pl.ds(f * LOC, LOC)
             result = disperse(
                 u, t, "fwd_native" if e == 0 else "fwd_apart", "inv_native" if e == 3 else "inv_apart",
@@ -456,23 +441,33 @@
         for k in range(1, 8):
             near_copy(e, k).start()
 
-    def gather(j):
+    def gather(step, j, first, last):
         def one(k, carry):
-            send_items[j, k] = own[j, pl.ds(slot_item[16 * j + k] * 4, 4)]
+            send_items[j, k] = own[step, pl.ds(slot_item[16 * j + k] * 4, 4)]
             return carry
 
-        lax.fori_loop(0, WAVE, one, 0)
-        (first_own if j == 0 else slot_own)[16 * j] = send_items[j, 0]
+        lax.fori_loop(first, last, one, 0)
+
+    def straight_edges():
+        def one(k, carry):
+            send_edge[0, k], send_edge[1, k] = edges(send_items[0, 8 + k])
+            return carry
+
+        lax.fori_loop(0, 8, one, 0)
+        for side, here in ((0, is_last), (1, is_first)):
+
+            @pl.when(here > 0)
+            def _(side=side):
+                for k in range(8):
+                    first_copy(side, k, True).start()
 
     def forward_first(k):
         first_edge[0, k], first_edge[1, k] = edges(first_own[k])
-        first_copy(0, k).start()
-        first_copy(1, k).start()
-
-    def forward_second(k):
-        slot_edge[0, 16 + k], slot_edge[1, 16 + k] = edges(slot_own[16 + k])
-        second_copy(0, k).start()
-        second_copy(1, k).start()
+        for side, here in ((0, is_last), (1, is_first)):
+
+            @pl.when(here == 0)
+            def _(side=side):
+                first_copy(side, k).start()
 
     def first_slots(g, carry):
         blocks = []
@@ -480,20 +475,15 @@
             k = g * 4 + i
             first_copy(0, k).wait_recv()
             first_copy(1, k).wait_recv()
-            fibre = lax.div(slot_from[k], 4)
+            fibre = lax.div(slot_from[8 + k], 4)
             parts = [first_halo[0, k], first_own[k], first_halo[1, k]]
             blocks.append(turned(parts, BLK, 0, fibre, nonlin[0, fibre] * (1.0 / CH)))
         table = pl.ds(g * LOC, LOC)
         result = disperse(
             jnp.concatenate(blocks, axis=0), t, "fwd_apart", "inv_apart", slot_fc[table], slot_fs[table]
         )
-        slots = pl.ds(g * 4, 4)
+        slots = pl.ds(8 + g * 4, 4)
         slot_own[slots] = result.reshape(4, 4, 16, 128)
-        up, down = edges(result)
-        slot_edge[0, slots] = up.reshape(4, 4, 8, 128)
-        slot_edge[1, slots] = down.reshape(4, 4, 8, 128)
-        group_copy(0, g).start()
-        group_copy(1, g).start()
         return carry
 
     def finish_near(e):
@@ -520,38 +510,47 @@
 
     lax.fori_loop(0, FIB, start_halo, 0)
     fill_tables(1)
-    lax.fori_loop(0, WAVE, fill_slots, 0)
+    lax.fori_loop(0, 8, fill_slots, 0)
     run_step(0, True)
-    gather(0)
-    item_copy(0, 8).start()
+    gather(0, 0, 8, 16)
     finish_near(0)
-    order = (9, 10, 11, 12, 13, 14, 15, 1, 2, 3, 4, 5, 6, 7)
-    for k in order:
+    straight_edges()
+    for k in range(8, 16):
         item_copy(0, k).start()
     finish_far(0, True)
     run_step(1, False)
-    gather(1)
+    gather(1, 1, 0, 16)
     item_copy(1, 8).start()
+    gather(1, 0, 0, 8)
     finish_near(1)
-    for k in order:
+    for k in range(9, 16):
         item_copy(1, k).start()
-
-    forward_first(0)
-    for k in (1, 2, 3, 4, 5, 6, 7, 8, 9, 10, 11, 12, 13, 14, 15):
+    for k in range(1, 8):
+        item_copy(0, k).start()
+        item_copy(1, k).start()
+    slot_own[0] = send_items[0, 0]
+    slot_own[16] = send_items[1, 0]
+
+    for k in range(8, 16):
         item_copy(0, k).wait_recv()
-        forward_first(k)
-    forward_second(0)
-    lax.fori_loop(0, 4, first_slots, 0)
-    finish_far(1, True)
-    for k in (1, 2, 3, 4, 5, 6, 7, 8, 9, 10, 11, 12, 13, 14, 15):
+        forward_first(k - 8)
+    lax.fori_loop(0, 2, first_slots, 0)
+    finish_far(1, False)
+    for k in range(1, 8):
+        item_copy(0, k).wait_recv()
+    for k in range(1, 16):
         item_copy(1, k).wait_recv()
-        forward_second(k)
-    for g in range(4):
-        group_copy(0, g).wait_recv()
-        group_copy(1, g).wait_recv()
-    for k in range(16):
-        second_copy(0, k).wait_recv()
-        second_copy(1, k).wait_recv()
+
+    def place_fibre(f, carry):
+        for i in range(4):
+            fibre = take_fibre[f * 4 + i]
+            u = slot_own[take[f * 4 + i]].reshape(2, 2, 16, 128)
+            u = rotate_apart(u, total[1, fibre], nonlin[0, fibre] * (1.0 / CH))
+            own[1, pl.ds(f * 16 + i * 4, 4)] = u.reshape(4, 16, 128)
+        keep_edges(1, f, own[1, pl.ds(f * 16, 16)])
+        return carry
+
+    lax.fori_loop(0, FIB, place_fibre, 0)
 
     run_step(2, True)
     finish_near(2)
@@ -577,7 +576,7 @@
     lax.fori_loop(0, FIB, last, 0)
 
     def drain_halo(f, carry):
-        for e in (0, 1, 3):
+        for e in range(4):
             halo_copy(e, 0, f).wait_send()
             halo_copy(e, 1, f).wait_send()
         return carry
@@ -587,18 +586,15 @@
         for k in range(1, 8):
             near_copy(e, k).wait_send()
         far_copy(e).wait_send()
-    for e in range(3):
+    for e in (0, 2):
         side_copy(e, 0).wait_send()
         side_copy(e, 1).wait_send()
     for k in range(1, 16):
         item_copy(0, k).wait_send()
         item_copy(1, k).wait_send()
     for side in range(2):
-        for k in range(16):
+        for k in range(8):
             first_copy(side, k).wait_send()
-            second_copy(side, k).wait_send()
-        for g in range(4):
-            group_copy(side, g).wait_send()
     for f in range(FIB):
         store(f).wait()
 
@@ -633,16 +629,14 @@
             pltpu.VMEM((4, FIB, 8, 128), F32),
             pltpu.VMEM((2, FIB, 8, 128), F32),
             pltpu.VMEM((2, FIB, 8, 128), F32),
-            pltpu.VMEM((2, FIB, 8, 128), F32),
             pltpu.VMEM((2, WAVE, 4, 16, 128), F32),
-            pltpu.VMEM((WAVE, 4, 16, 128), F32),
-            pltpu.VMEM((2, WAVE, 4, 8, 128), F32),
-            pltpu.VMEM((2, WAVE, 4, 8, 128), F32),
+            pltpu.VMEM((2, 8, 4, 8, 128), F32),
+            pltpu.VMEM((8, 4, 16, 128), F32),
+            pltpu.VMEM((2, 8, 4, 8, 128), F32),
+            pltpu.VMEM((2, 8, 4, 8, 128), F32),
             pltpu.VMEM((2 * WAVE, 4, 16, 128), F32),
-            pltpu.VMEM((2, 2 * WAVE, 4, 8, 128), F32),
-            pltpu.VMEM((2, 2 * WAVE, 4, 8, 128), F32),
-            pltpu.VMEM((2 * WAVE, 16, 128), F32),
-            pltpu.VMEM((2 * WAVE, 16, 128), F32),
+            pltpu.VMEM((WAVE, 16, 128), F32),
+            pltpu.VMEM((WAVE, 16, 128), F32),
             pltpu.SMEM((2 * WAVE,), jnp.int32),
             pltpu.SMEM((WAVE,), jnp.int32),
             pltpu.SMEM((WAVE,), jnp.int32),
@@ -653,9 +647,7 @@
             dma((4,)), dma((4,)),
             dma((4, 2)), dma((4, 2)),
             dma((2, WAVE)), dma((2, WAVE)),
-            dma((2, WAVE)), dma((2, WAVE)),
-            dma((2, FIB)), dma((2, FIB)),
-            dma((2, WAVE)), dma((2, WAVE)),
+            dma((2, 8)), dma((2, 8)),
         ],
         compiler_params=pltpu.CompilerParams(
             collective_id=0, has_side_effects=True, vmem_limit_bytes=67043328

time: 157 us -> 154 us (0.981)
  Pallas kernels: 155 us -> 152 us
    pallas_call x1, Pallas kernels: 155 us -> 152 us  [local(): pl.pallas_call(kernel, out_shape=jax.ShapeDtypeStruct((SEQ, 16, 128), F32...]
where the time goes in v3:
time: 154 us
  Pallas kernels  152 us (99%)
  local copies, waits for them, and re-layouts  1.87 us (1%)
    pallas_call x1, Pallas kernels, local(): pl.pallas_call(kernel, out_shape=jax.ShapeDtypeStruct((SEQ, 16, 128), F32...  152 us

profile of v3, /device:TPU:1, one launch (start us, length us, event | category | flops | bytes accessed | tf_op | source)
XLA Modules:
  0.0 153.5 jit_solution(14258574008882601325)
XLA Ops:
  0.0 151.7 %propagate.1 = f32[64,16,128]{2,1,0:T(8,128)} custom-call(s32[4]{0:T(128)} %lit.1, f32[2,4]{1,0:T(2,128)} %disp.1, f32[2,4]{1,0:T(2,128)} %nonlin.1, s32[4,64]{1,0:T(4,128)} %fibre_hbm.1, s32[4,64]{1,0:T(4,128)} %slot_hbm.1, f32[64,16,128]{2,1,0:T(8,128)} %bitcast.11, bf16[10,256,256]{2,1,0:T(8,128)(2,1)} %constant.4.clone.wide_hbm, ...), custom_call_target="tpu_custom_call" | custom-call | tf_op jit(solution)/shard_map/propagate/pallas_call | solution.py:608
  151.7 1.9 %copy.12 = f32[4,8,2,2,1024]{4,3,2,1,0:T(2,128)} copy(f32[4,8,2,2,1024]{4,3,2,1,0:T(2,128)} %bitcast.10) | data formatting | bytes 1048576

commit v4 on v1

--- a/solution.py
+++ b/solution.py
@@ -175,39 +175,43 @@
 
 
 def disperse(u, t, fwd, inv, filt_cos, filt_sin):
-    rows = u.reshape(512, 128)
-    x = jnp.concatenate([rows[:256], rows[256:]], axis=1)
+    eights = u.shape[0] // 8
+    rows = u.reshape(eights, 256, 128)
+    x = jnp.concatenate([rows[h] for h in range(eights)], axis=1)
     y = left_product(t[fwd], x)
     tc = jnp.broadcast_to(t["twist_cos"][...][None], (8, 16, 128)).reshape(128, 128)
     ts = jnp.broadcast_to(t["twist_sin"][...][None], (8, 16, 128)).reshape(128, 128)
     halves = []
-    for h in range(2):
+    for h in range(eights):
         re = y[:128, h * 128 : (h + 1) * 128]
         im = y[128:, h * 128 : (h + 1) * 128]
         halves.append(jnp.concatenate([re * tc + im * ts, im * tc - re * ts], axis=1))
     spectrum = right_product(jnp.concatenate(halves, axis=0), t["col_fwd"])
     sr, si = spectrum[:, :128], spectrum[:, 128:]
-    fc = jnp.broadcast_to(filt_cos[:, None], (8, 2, 16, 128)).reshape(256, 128)
-    fs = jnp.broadcast_to(filt_sin[:, None], (8, 2, 16, 128)).reshape(256, 128)
+    channels = eights * 4
+    fc = jnp.broadcast_to(filt_cos[:, None], (channels, 2, 16, 128)).reshape(eights * 128, 128)
+    fs = jnp.broadcast_to(filt_sin[:, None], (channels, 2, 16, 128)).reshape(eights * 128, 128)
     shaped = jnp.concatenate([sr * fc - si * fs, sr * fs + si * fc], axis=1)
     back = right_product(shaped, t["col_inv"])
     br, bi = back[:, :128], back[:, 128:]
     parts = []
-    for h in range(2):
+    for h in range(eights):
         re, im = br[h * 128 : (h + 1) * 128], bi[h * 128 : (h + 1) * 128]
         parts.append(jnp.concatenate([re * tc - im * ts, re * ts + im * tc], axis=0))
     out = left_product(t[inv], jnp.concatenate(parts, axis=1))
-    return jnp.concatenate([out[:, :128], out[:, 128:]], axis=0).reshape(16, 16, 128)
+    return jnp.concatenate([out[:, h * 128 : (h + 1) * 128] for h in range(eights)], axis=0).reshape(
+        eights * 8, 16, 128
+    )
 
 
 def kernel(
     lit, disp, nonlin, fibre_hbm, slot_hbm, field_hbm, wide_hbm, twist_hbm,
-    out_hbm,
-    wide, twist, route_f, route_s, launch, result_buf,
+    out_hbm, total_hbm,
+    wide, twist, route_f, route_s, launch,
     filt_c, filt_s, halo, own, edge, pack, near, far, half_sum, total, q_side,
     send_items, recv_items, slot_item, take, take_fibre,
     load_s, out_s,
-    halo_ss, halo_rs, near_ss, near_rs, far_ss, far_rs, side_ss, side_rs, item_ss, item_rs,
+    halo_ss, halo_rs, near_ss, near_rs, far_ss, far_rs, side_ss, side_rs, item_ss, item_rs, vouch,
 ):
     t = dict(
         fwd_native=(wide.at[0], wide.at[1]), fwd_apart=(wide.at[2], wide.at[3]),
@@ -233,9 +237,12 @@
     d_right, d_left = (me, right), (me, left)
 
     barrier = pltpu.get_barrier_semaphore()
-    for k in range(1, 16):
+    upper = at // 16
+    z_up = (lax.rem(me + 8 * upper, WAVE), lax.rem(at + 16, TM))
+    z_down = (lax.rem(me + 8 * (1 - upper), WAVE), lax.rem(at + 16, TM))
+    for k in range(1, 8):
         pl.semaphore_signal(barrier, inc=1, device_id=(mate(k), at), device_id_type=MESH)
-    for target in (d_right, d_left, q_right, q_left):
+    for target in (d_right, d_left, q_right, q_left, z_up, z_down):
         pl.semaphore_signal(barrier, inc=1, device_id=target, device_id_type=MESH)
     loads = [
         pltpu.make_async_copy(src, dst, load_s.at[i])
@@ -296,7 +303,8 @@
     fill_tables(0)
     for load in loads:
         load.wait()
-    pl.semaphore_wait(barrier, 19)
+    pl.semaphore_wait(barrier, 13)
+    pl.semaphore_signal(vouch.at[0], inc=1, device_id=z_up, device_id_type=MESH)
 
     def halo_copy(e, side, f):
         group = pl.ds(f * 16, 16)
@@ -348,7 +356,7 @@
     def run_step(e, send_halo):
         span = e // 2
 
-        def body(f, carry):
+        def fetch(f):
             halo_copy(e, 0, f).wait_recv()
             halo_copy(e, 1, f).wait_recv()
             group = pl.ds(f * 16, 16)
@@ -371,28 +379,36 @@
             if e == 0:
                 channel = me * LOC + lax.broadcasted_iota(jnp.int32, (16, 1, 128), 0) // 2
                 u = jnp.where(channel < lit[f], u, 0.0)
-            table = pl.ds(f * LOC, LOC)
-            result = disperse(
-                u, t, "fwd_native" if e == 0 else "fwd_apart", "inv_native" if e == 3 else "inv_apart",
-                filt_c[span, table], filt_s[span, table],
-            )
-            own[e, group] = result
+            return u
+
+        def keep(f, result):
+            own[e, pl.ds(f * 16, 16)] = result
             if send_halo:
                 keep_edges(e, f, result)
             both = jnp.sum(result * result, axis=0)
-            if e < 3:
-                pack[e, f] = both[:8] + both[8:]
-            else:
-                full = both + swap(both)
-                even = even_rows()
-                row = f // 2 * 2
-                for h in range(2):
-                    part = full[h * 8 : h * 8 + 8]
-                    old = pack[e, row + h]
-                    pack[e, row + h] = jnp.where(even, jnp.where(lax.rem(f, 2) == 0, part, old), part)
-            return carry
-
-        lax.fori_loop(0, FIB, body, 0)
+            return both[:8] + both[8:] if e < 3 else both + swap(both)
+
+        fwd = "fwd_native" if e == 0 else "fwd_apart"
+        inv = "inv_native" if e == 3 else "inv_apart"
+        if e in (1, 3):
+            u = jnp.concatenate([fetch(f) for f in range(FIB)], axis=0)
+            result = disperse(u, t, fwd, inv, filt_c[span], filt_s[span])
+            powers = [keep(f, result[f * 16 : f * 16 + 16]) for f in range(FIB)]
+            for f in range(FIB):
+                if e == 1:
+                    pack[e, f] = powers[f]
+                else:
+                    j, h = f // 2 * 2, f % 2
+                    rows = slice(h * 8, h * 8 + 8)
+                    pack[e, f] = jnp.where(even_rows(), powers[j][rows], powers[j + 1][rows])
+        else:
+
+            def body(f, carry):
+                table = pl.ds(f * LOC, LOC)
+                pack[e, f] = keep(f, disperse(fetch(f), t, fwd, inv, filt_c[span, table], filt_s[span, table]))
+                return carry
+
+            lax.fori_loop(0, FIB, body, 0)
         for k in range(1, 8):
             near_copy(e, k).start()
 
@@ -419,9 +435,12 @@
         return carry
 
     lax.fori_loop(0, FIB, start_halo, 0)
-    run_step(0, True)
     fill_tables(1)
     plan_switch()
+    pl.semaphore_wait(vouch.at[0], 1)
+    pl.semaphore_signal(vouch.at[1], inc=1, device_id=z_up, device_id_type=MESH)
+    run_step(0, True)
+    pl.semaphore_wait(vouch.at[1], 1)
     finish_near(0)
     finish_far(0, True)
     run_step(1, False)
@@ -430,12 +449,16 @@
         send_items[s] = own[1, pl.ds(slot_item[s] * 4, 4)]
         return carry
 
-    lax.fori_loop(0, 2 * WAVE, gather, 0)
-    item_copy(8).start()
-    finish_near(1)
-    for k in (9, 10, 11, 12, 13, 14, 15, 1, 2, 3, 4, 5, 6, 7):
+    lax.fori_loop(WAVE, 2 * WAVE, gather, 0)
+    for k in (8, 9, 10, 11, 12, 13):
+        item_copy(k).start()
+    lax.fori_loop(0, WAVE, gather, 0)
+    for k in (1, 2, 3, 4, 5, 6, 7):
         item_copy(k).start()
     recv_items[0:2] = send_items[0:2]
+    finish_near(1)
+    for k in (14, 15):
+        item_copy(k).start()
     finish_far(1, False)
     for k in range(1, 16):
         item_copy(k).wait_recv()
@@ -459,24 +482,12 @@
     finish_near(2)
     finish_far(2, True)
     run_step(3, False)
+    result_store = pltpu.make_async_copy(own.at[3], out_hbm, out_s.at[0])
+    result_store.start()
     finish_near(3)
     finish_far(3, False)
-
-    def store(f):
-        group = pl.ds(f * 16, 16)
-        return pltpu.make_async_copy(result_buf.at[group], out_hbm.at[group], out_s.at[f])
-
-    def last(f, carry):
-        group = pl.ds(f * 16, 16)
-        u = own[3, group].reshape(8, 2, 16, 128)
-        first, second = unpack_pair(total[3, pl.ds(f // 2 * 2, 2)].reshape(16, 128))
-        q = jnp.where(lax.rem(f, 2) == 0, first, second)
-        u = rotate_native(u, q, nonlin[1, f] * (1.0 / CH))
-        result_buf[group] = u.reshape(16, 16, 128)
-        store(f).start()
-        return carry
-
-    lax.fori_loop(0, FIB, last, 0)
+    total_store = pltpu.make_async_copy(total.at[3], total_hbm, out_s.at[1])
+    total_store.start()
 
     def drain_halo(f, carry):
         for e in range(4):
@@ -494,8 +505,16 @@
         side_copy(e, 1).wait_send()
     for k in range(1, 16):
         item_copy(k).wait_send()
-    for f in range(FIB):
-        store(f).wait()
+    result_store.wait()
+    total_store.wait()
+
+
+def last_phase(nonlin, own, total, out):
+    f = pl.program_id(0)
+    first, second = unpack_pair(total[...].reshape(16, 128))
+    q = jnp.where(lax.rem(f, 2) == 0, first, second)
+    u = rotate_native(own[...].reshape(8, 2, 16, 128), q, nonlin[1, f] * (1.0 / CH))
+    out[...] = u.reshape(16, 16, 128)
 
 
 def local(field, lit_count, route_fibre, route_slot, dispersion, nonlinearity):
@@ -504,17 +523,19 @@
     smem = pl.BlockSpec(memory_space=pltpu.SMEM)
     hbm = pl.BlockSpec(memory_space=pltpu.HBM)
     dma = pltpu.SemaphoreType.DMA
-    result = pl.pallas_call(
+    field_out, total_out = pl.pallas_call(
         kernel,
-        out_shape=jax.ShapeDtypeStruct((SEQ, 16, 128), F32),
+        out_shape=[
+            jax.ShapeDtypeStruct((SEQ, 16, 128), F32),
+            jax.ShapeDtypeStruct((FIB, 8, 128), F32),
+        ],
         in_specs=[smem] * 3 + [hbm] * 5,
-        out_specs=hbm,
+        out_specs=[hbm, hbm],
         scratch_shapes=[
             pltpu.VMEM((10, 256, 256), BF16),
             pltpu.VMEM((2, 16, 128), F32),
             pltpu.VMEM((FIB, 64), jnp.int32),
             pltpu.VMEM((FIB, 64), jnp.int32),
-            pltpu.VMEM((SEQ, 16, 128), F32),
             pltpu.VMEM((SEQ, 16, 128), F32),
             pltpu.VMEM((2, FIB * LOC, 16, 128), F32),
             pltpu.VMEM((2, FIB * LOC, 16, 128), F32),
@@ -532,18 +553,27 @@
             pltpu.SMEM((2 * WAVE,), jnp.int32),
             pltpu.SMEM((WAVE,), jnp.int32),
             pltpu.SMEM((WAVE,), jnp.int32),
-            dma((5,)), dma((FIB,)),
+            dma((5,)), dma((2,)),
             dma((4, 2, FIB)), dma((4, 2, FIB)),
             dma((4, 8)), dma((4, 8)),
             dma((4,)), dma((4,)),
             dma((4, 2)), dma((4, 2)),
-            dma((WAVE,)), dma((WAVE,)),
+            dma((WAVE,)), dma((WAVE,)), pltpu.SemaphoreType.REGULAR((2,)),
         ],
         compiler_params=pltpu.CompilerParams(
             collective_id=0, has_side_effects=True, vmem_limit_bytes=67043328
         ),
         name="propagate",
     )(lit_count, dispersion, nonlinearity, route_fibre, route_slot, rows, wide, twist)
+    block = pl.BlockSpec((16, 16, 128), lambda f: (f, 0, 0))
+    result = pl.pallas_call(
+        last_phase,
+        grid=(FIB,),
+        out_shape=jax.ShapeDtypeStruct((SEQ, 16, 128), F32),
+        in_specs=[smem, block, pl.BlockSpec((2, 8, 128), lambda f: (f // 2, 0, 0))],
+        out_specs=block,
+        name="last_phase",
+    )(nonlinearity, field_out, total_out)
     back = result.reshape(FIB, LOC, 2, 8, 2, 128).transpose(0, 1, 2, 4, 3, 5)
     return back.reshape(FIB, LOC, 2, 2, 1024)
 

time: 149 us -> 160 us (1.074)
  the two profiles are of different devices: /device:TPU:1 before, /device:TPU:374 now
where the time goes in v4:
time: 160 us
  Pallas kernels  160 us (100%)
    pallas_call x1, Pallas kernels, local(): pl.pallas_call(kernel, out_shape=[jax.ShapeDtypeStruct((SEQ, 16, 128), F3...  156 us
    pallas_call x1, Pallas kernels, local(): pl.pallas_call(last_phase, grid=(FIB,), out_shape=jax.ShapeDtypeStruct((S...  3.45 us

profile of v4, /device:TPU:374, one launch (start us, length us, event | category | flops | bytes accessed | tf_op | source)
XLA Modules:
  0.0 159.7 jit_solution(640155735827729014)
XLA Ops:
  0.0 156.3 %propagate.1 = (f32[64,16,128]{2,1,0:T(8,128)}, f32[4,8,128]{2,1,0:T(8,128)}) custom-call(s32[4]{0:T(128)} %lit.1, f32[2,4]{1,0:T(2,128)} %disp.1, f32[2,4]{1,0:T(2,128)} %nonlin.3, s32[4,64]{1,0:T(4,128)} %fibre_hbm.1, s32[4,64]{1,0:T(4,128)} %slot_hbm.1, f32[64,16,128]{2,1,0:T(8,128)} %bitcast.10, bf16[10,256,256]{2,1,0:T(8,128)(2,1)} %constant.4.clone.wide_hbm, ...), custom_call_target="tpu_custom_call" | custom-call | tf_op jit(solution)/shard_map/propagate/pallas_call | solution.py:526
  156.3 3.4 %last_phase.1 = f32[64,16,128]{2,1,0:T(8,128)} custom-call(f32[2,4]{1,0:T(2,128)} %nonlin.3, f32[64,16,128]{2,1,0:T(8,128)} %get-tuple-element.7.own, f32[4,8,128]{2,1,0:T(8,128)} %get-tuple-element.8.total), custom_call_target="tpu_custom_call" | custom-call | tf_op jit(solution)/shard_map/last_phase/pallas_call | solution.py:569

commit v5 on v4

--- a/solution.py
+++ b/solution.py
@@ -206,12 +206,12 @@
 
 def kernel(
     lit, disp, nonlin, fibre_hbm, slot_hbm, field_hbm, wide_hbm, twist_hbm,
-    out_hbm, total_hbm,
-    wide, twist, route_f, route_s, launch,
+    out_hbm,
+    wide, twist, route_f, route_s, launch, result_buf,
     filt_c, filt_s, halo, own, edge, pack, near, far, half_sum, total, q_side,
     send_items, recv_items, slot_item, take, take_fibre,
     load_s, out_s,
-    halo_ss, halo_rs, near_ss, near_rs, far_ss, far_rs, side_ss, side_rs, item_ss, item_rs, vouch,
+    halo_ss, halo_rs, near_ss, near_rs, far_ss, far_rs, side_ss, side_rs, item_ss, item_rs, vouch, column,
 ):
     t = dict(
         fwd_native=(wide.at[0], wide.at[1]), fwd_apart=(wide.at[2], wide.at[3]),
@@ -242,7 +242,16 @@
     z_down = (lax.rem(me + 8 * (1 - upper), WAVE), lax.rem(at + 16, TM))
     for k in range(1, 8):
         pl.semaphore_signal(barrier, inc=1, device_id=(mate(k), at), device_id_type=MESH)
-    for target in (d_right, d_left, q_right, q_left, z_up, z_down):
+    my_high = my_z * 8 + at // 4
+
+    def along_z(step):
+        high = lax.rem(my_high + step + 16, 16)
+        return (lax.div(high, 8) * 8 + lax.rem(me, 8), lax.rem(high, 8) * 4 + lax.rem(at, 4))
+
+    first_round = [along_z(step) for step in (-5, 5)]
+    second_round = [along_z(step) for step in (-2, -1, 1, 2, 3)]
+    answers = [along_z(-3)]
+    for target in (d_right, d_left, q_right, q_left, z_up, z_down, *first_round, *second_round, *answers):
         pl.semaphore_signal(barrier, inc=1, device_id=target, device_id_type=MESH)
     loads = [
         pltpu.make_async_copy(src, dst, load_s.at[i])
@@ -303,7 +312,7 @@
     fill_tables(0)
     for load in loads:
         load.wait()
-    pl.semaphore_wait(barrier, 13)
+    pl.semaphore_wait(barrier, 21)
     pl.semaphore_signal(vouch.at[0], inc=1, device_id=z_up, device_id_type=MESH)
 
     def halo_copy(e, side, f):
@@ -360,26 +369,45 @@
             halo_copy(e, 0, f).wait_recv()
             halo_copy(e, 1, f).wait_recv()
             group = pl.ds(f * 16, 16)
-            parts = [halo[e, 0, group], launch[group] if e == 0 else own[e - 1, group], halo[e, 1, group]]
-            if e in (1, 3):
-                gain = nonlin[span, f] * (1.0 / CH)
-                low = low_rows()
-                before, after = q_side[e - 1, 0, f], q_side[e - 1, 1, f]
-                sums = (
-                    jnp.where(low, turn(before, 4), before),
-                    total[e - 1, f],
-                    jnp.where(low, after, turn(after, 4)),
-                )
-                turns = (rotate_edge, rotate_apart, rotate_edge)
-                parts = [
-                    rule(part.reshape(8, 2, *part.shape[1:]), q, gain).reshape(part.shape)
-                    for rule, part, q in zip(turns, parts, sums)
-                ]
-            u = jnp.concatenate(parts, axis=1)
+            middle = launch[group] if e == 0 else own[e - 1, group]
+            u = jnp.concatenate([halo[e, 0, group], middle, halo[e, 1, group]], axis=1)
             if e == 0:
                 channel = me * LOC + lax.broadcasted_iota(jnp.int32, (16, 1, 128), 0) // 2
                 u = jnp.where(channel < lit[f], u, 0.0)
             return u
+
+        def turned(rule, part, f, q):
+            gain = nonlin[span, f] * (1.0 / CH)
+            return rule(part.reshape(8, 2, *part.shape[1:]), q, gain).reshape(part.shape)
+
+        def fetch_turned():
+            middle = []
+            for f in range(FIB):
+                middle.append(turned(rotate_apart, own[e - 1, pl.ds(f * 16, 16)], f, total[e - 1, f]))
+            side_copy(e - 1, 0).wait_recv()
+            side_copy(e - 1, 1).wait_recv()
+            if e == 1:
+                pl.semaphore_wait(column.at[0], 2)
+                for target in second_round:
+                    pl.semaphore_signal(column.at[1], inc=1, device_id=target, device_id_type=MESH)
+            low = low_rows()
+            parts = []
+            for f in range(FIB):
+                group = pl.ds(f * 16, 16)
+                before, after = q_side[e - 1, 0, f], q_side[e - 1, 1, f]
+                halo_copy(e, 0, f).wait_recv()
+                halo_copy(e, 1, f).wait_recv()
+                parts.append(
+                    jnp.concatenate(
+                        [
+                            turned(rotate_edge, halo[e, 0, group], f, jnp.where(low, turn(before, 4), before)),
+                            middle[f],
+                            turned(rotate_edge, halo[e, 1, group], f, jnp.where(low, after, turn(after, 4))),
+                        ],
+                        axis=1,
+                    )
+                )
+            return jnp.concatenate(parts, axis=0)
 
         def keep(f, result):
             own[e, pl.ds(f * 16, 16)] = result
@@ -391,8 +419,7 @@
         fwd = "fwd_native" if e == 0 else "fwd_apart"
         inv = "inv_native" if e == 3 else "inv_apart"
         if e in (1, 3):
-            u = jnp.concatenate([fetch(f) for f in range(FIB)], axis=0)
-            result = disperse(u, t, fwd, inv, filt_c[span], filt_s[span])
+            result = disperse(fetch_turned(), t, fwd, inv, filt_c[span], filt_s[span])
             powers = [keep(f, result[f * 16 : f * 16 + 16]) for f in range(FIB)]
             for f in range(FIB):
                 if e == 1:
@@ -423,11 +450,12 @@
     def finish_far(e, sides):
         far_copy(e).wait_recv()
         total[e] = half_sum[e] + far[e]
+        if e == 0:
+            for target in first_round:
+                pl.semaphore_signal(column.at[0], inc=1, device_id=target, device_id_type=MESH)
         if sides:
             side_copy(e, 0).start()
             side_copy(e, 1).start()
-            side_copy(e, 0).wait_recv()
-            side_copy(e, 1).wait_recv()
 
     def start_halo(f, carry):
         halo_copy(0, 0, f).start()
@@ -450,6 +478,7 @@
         return carry
 
     lax.fori_loop(WAVE, 2 * WAVE, gather, 0)
+    pl.semaphore_wait(column.at[1], 5)
     for k in (8, 9, 10, 11, 12, 13):
         item_copy(k).start()
     lax.fori_loop(0, WAVE, gather, 0)
@@ -482,12 +511,24 @@
     finish_near(2)
     finish_far(2, True)
     run_step(3, False)
-    result_store = pltpu.make_async_copy(own.at[3], out_hbm, out_s.at[0])
-    result_store.start()
     finish_near(3)
     finish_far(3, False)
-    total_store = pltpu.make_async_copy(total.at[3], total_hbm, out_s.at[1])
-    total_store.start()
+
+    def store(f):
+        group = pl.ds(f * 16, 16)
+        return pltpu.make_async_copy(result_buf.at[group], out_hbm.at[group], out_s.at[f])
+
+    def last(f, carry):
+        group = pl.ds(f * 16, 16)
+        u = own[3, group].reshape(8, 2, 16, 128)
+        first, second = unpack_pair(total[3, pl.ds(f // 2 * 2, 2)].reshape(16, 128))
+        q = jnp.where(lax.rem(f, 2) == 0, first, second)
+        u = rotate_native(u, q, nonlin[1, f] * (1.0 / CH))
+        result_buf[group] = u.reshape(16, 16, 128)
+        store(f).start()
+        return carry
+
+    lax.fori_loop(0, FIB, last, 0)
 
     def drain_halo(f, carry):
         for e in range(4):
@@ -505,16 +546,8 @@
         side_copy(e, 1).wait_send()
     for k in range(1, 16):
         item_copy(k).wait_send()
-    result_store.wait()
-    total_store.wait()
-
-
-def last_phase(nonlin, own, total, out):
-    f = pl.program_id(0)
-    first, second = unpack_pair(total[...].reshape(16, 128))
-    q = jnp.where(lax.rem(f, 2) == 0, first, second)
-    u = rotate_native(own[...].reshape(8, 2, 16, 128), q, nonlin[1, f] * (1.0 / CH))
-    out[...] = u.reshape(16, 16, 128)
+    for f in range(FIB):
+        store(f).wait()
 
 
 def local(field, lit_count, route_fibre, route_slot, dispersion, nonlinearity):
@@ -523,19 +556,17 @@
     smem = pl.BlockSpec(memory_space=pltpu.SMEM)
     hbm = pl.BlockSpec(memory_space=pltpu.HBM)
     dma = pltpu.SemaphoreType.DMA
-    field_out, total_out = pl.pallas_call(
+    result = pl.pallas_call(
         kernel,
-        out_shape=[
-            jax.ShapeDtypeStruct((SEQ, 16, 128), F32),
-            jax.ShapeDtypeStruct((FIB, 8, 128), F32),
-        ],
+        out_shape=jax.ShapeDtypeStruct((SEQ, 16, 128), F32),
         in_specs=[smem] * 3 + [hbm] * 5,
-        out_specs=[hbm, hbm],
+        out_specs=hbm,
         scratch_shapes=[
             pltpu.VMEM((10, 256, 256), BF16),
             pltpu.VMEM((2, 16, 128), F32),
             pltpu.VMEM((FIB, 64), jnp.int32),
             pltpu.VMEM((FIB, 64), jnp.int32),
+            pltpu.VMEM((SEQ, 16, 128), F32),
             pltpu.VMEM((SEQ, 16, 128), F32),
             pltpu.VMEM((2, FIB * LOC, 16, 128), F32),
             pltpu.VMEM((2, FIB * LOC, 16, 128), F32),
@@ -553,27 +584,19 @@
             pltpu.SMEM((2 * WAVE,), jnp.int32),
             pltpu.SMEM((WAVE,), jnp.int32),
             pltpu.SMEM((WAVE,), jnp.int32),
-            dma((5,)), dma((2,)),
+            dma((5,)), dma((FIB,)),
             dma((4, 2, FIB)), dma((4, 2, FIB)),
             dma((4, 8)), dma((4, 8)),
             dma((4,)), dma((4,)),
             dma((4, 2)), dma((4, 2)),
             dma((WAVE,)), dma((WAVE,)), pltpu.SemaphoreType.REGULAR((2,)),
+            pltpu.SemaphoreType.REGULAR((2,)),
         ],
         compiler_params=pltpu.CompilerParams(
             collective_id=0, has_side_effects=True, vmem_limit_bytes=67043328
         ),
         name="propagate",
     )(lit_count, dispersion, nonlinearity, route_fibre, route_slot, rows, wide, twist)
-    block = pl.BlockSpec((16, 16, 128), lambda f: (f, 0, 0))
-    result = pl.pallas_call(
-        last_phase,
-        grid=(FIB,),
-        out_shape=jax.ShapeDtypeStruct((SEQ, 16, 128), F32),
-        in_specs=[smem, block, pl.BlockSpec((2, 8, 128), lambda f: (f // 2, 0, 0))],
-        out_specs=block,
-        name="last_phase",
-    )(nonlinearity, field_out, total_out)
     back = result.reshape(FIB, LOC, 2, 8, 2, 128).transpose(0, 1, 2, 4, 3, 5)
     return back.reshape(FIB, LOC, 2, 2, 1024)
 

time: 160 us -> 146 us (0.912)
  the two profiles are of different devices: /device:TPU:374 before, /device:TPU:1 now
where the time goes in v5:
time: 146 us; the launch traced here: 144 us
  Pallas kernels  142 us (97%)
  local copies, waits for them, and re-layouts  1.87 us (1%)
    pallas_call x1, Pallas kernels, local(): pl.pallas_call(kernel, out_shape=jax.ShapeDtypeStruct((SEQ, 16, 128), F32...  142 us

profile of v5, /device:TPU:1, one launch (start us, length us, event | category | flops | bytes accessed | tf_op | source)
XLA Modules:
  0.0 144.1 jit_solution(100471776569339250)
XLA Ops:
  0.0 142.2 %propagate.1 = f32[64,16,128]{2,1,0:T(8,128)} custom-call(s32[4]{0:T(128)} %lit.1, f32[2,4]{1,0:T(2,128)} %disp.1, f32[2,4]{1,0:T(2,128)} %nonlin.1, s32[4,64]{1,0:T(4,128)} %fibre_hbm.1, s32[4,64]{1,0:T(4,128)} %slot_hbm.1, f32[64,16,128]{2,1,0:T(8,128)} %bitcast.11, bf16[10,256,256]{2,1,0:T(8,128)(2,1)} %constant.4.clone.wide_hbm, ...), custom_call_target="tpu_custom_call" | custom-call | tf_op jit(solution)/shard_map/propagate/pallas_call | solution.py:559
  142.2 1.9 %copy.12 = f32[4,8,2,2,1024]{4,3,2,1,0:T(2,128)} copy(f32[4,8,2,2,1024]{4,3,2,1,0:T(2,128)} %bitcast.10) | data formatting | bytes 1048576

commit v6 on v5

--- a/solution.py
+++ b/solution.py
@@ -330,16 +330,18 @@
             device_id_type=MESH,
         )
 
-    def near_copy(e, k):
+    def near_copy(e, h, k):
+        half = pl.ds(2 * h, 2)
         return pltpu.make_async_remote_copy(
-            src_ref=pack.at[e], dst_ref=near.at[e, k], send_sem=near_ss.at[e, k],
-            recv_sem=near_rs.at[e, k], device_id=(mate(k), at), device_id_type=MESH,
+            src_ref=pack.at[e, half], dst_ref=near.at[e, k, half], send_sem=near_ss.at[e, h, k],
+            recv_sem=near_rs.at[e, h, k], device_id=(mate(k), at), device_id_type=MESH,
         )
 
-    def far_copy(e):
+    def far_copy(e, h):
+        half = pl.ds(2 * h, 2)
         return pltpu.make_async_remote_copy(
-            src_ref=half_sum.at[e], dst_ref=far.at[e], send_sem=far_ss.at[e],
-            recv_sem=far_rs.at[e], device_id=(mate(8), at), device_id_type=MESH,
+            src_ref=half_sum.at[e, half], dst_ref=far.at[e, half], send_sem=far_ss.at[e, h],
+            recv_sem=far_rs.at[e, h], device_id=(mate(8), at), device_id_type=MESH,
         )
 
     def side_copy(e, side):
@@ -433,22 +435,33 @@
             def body(f, carry):
                 table = pl.ds(f * LOC, LOC)
                 pack[e, f] = keep(f, disperse(fetch(f), t, fwd, inv, filt_c[span, table], filt_s[span, table]))
+
+                @pl.when(lax.rem(f, 2) == 1)
+                def _():
+                    for k in range(1, 8):
+                        near_copy(e, lax.div(f, 2), k).start()
+
                 return carry
 
             lax.fori_loop(0, FIB, body, 0)
-        for k in range(1, 8):
-            near_copy(e, k).start()
+        if e in (1, 3):
+            for h in range(2):
+                for k in range(1, 8):
+                    near_copy(e, h, k).start()
 
     def finish_near(e):
-        acc = pack[e]
-        for k in range(1, 8):
-            near_copy(e, k).wait_recv()
-            acc = acc + near[e, k]
-        half_sum[e] = acc
-        far_copy(e).start()
+        for h in range(2):
+            half = pl.ds(2 * h, 2)
+            acc = pack[e, half]
+            for k in range(1, 8):
+                near_copy(e, h, k).wait_recv()
+                acc = acc + near[e, k, half]
+            half_sum[e, half] = acc
+            far_copy(e, h).start()
 
     def finish_far(e, sides):
-        far_copy(e).wait_recv()
+        far_copy(e, 0).wait_recv()
+        far_copy(e, 1).wait_recv()
         total[e] = half_sum[e] + far[e]
         if e == 0:
             for target in first_round:
@@ -512,6 +525,24 @@
     finish_far(2, True)
     run_step(3, False)
     finish_near(3)
+
+    def drain_halo(f, carry):
+        for e in range(4):
+            halo_copy(e, 0, f).wait_send()
+            halo_copy(e, 1, f).wait_send()
+        return carry
+
+    lax.fori_loop(0, FIB, drain_halo, 0)
+    for e in range(3):
+        for h in range(2):
+            for k in range(1, 8):
+                near_copy(e, h, k).wait_send()
+            far_copy(e, h).wait_send()
+    for e in (0, 2):
+        side_copy(e, 0).wait_send()
+        side_copy(e, 1).wait_send()
+    for k in range(1, 16):
+        item_copy(k).wait_send()
     finish_far(3, False)
 
     def store(f):
@@ -530,22 +561,10 @@
 
     lax.fori_loop(0, FIB, last, 0)
 
-    def drain_halo(f, carry):
-        for e in range(4):
-            halo_copy(e, 0, f).wait_send()
-            halo_copy(e, 1, f).wait_send()
-        return carry
-
-    lax.fori_loop(0, FIB, drain_halo, 0)
-    for e in range(4):
+    for h in range(2):
         for k in range(1, 8):
-            near_copy(e, k).wait_send()
-        far_copy(e).wait_send()
-    for e in (0, 2):
-        side_copy(e, 0).wait_send()
-        side_copy(e, 1).wait_send()
-    for k in range(1, 16):
-        item_copy(k).wait_send()
+            near_copy(3, h, k).wait_send()
+        far_copy(3, h).wait_send()
     for f in range(FIB):
         store(f).wait()
 
@@ -586,8 +605,8 @@
             pltpu.SMEM((WAVE,), jnp.int32),
             dma((5,)), dma((FIB,)),
             dma((4, 2, FIB)), dma((4, 2, FIB)),
-            dma((4, 8)), dma((4, 8)),
-            dma((4,)), dma((4,)),
+            dma((4, 2, 8)), dma((4, 2, 8)),
+            dma((4, 2)), dma((4, 2)),
             dma((4, 2)), dma((4, 2)),
             dma((WAVE,)), dma((WAVE,)), pltpu.SemaphoreType.REGULAR((2,)),
             pltpu.SemaphoreType.REGULAR((2,)),

time: 146 us -> 147 us (level); the launches traced: 144 us -> 147 us
  Pallas kernels: 142 us -> 145 us
    pallas_call x1, Pallas kernels: 142 us -> 145 us  [local(): pl.pallas_call(kernel, out_shape=jax.ShapeDtypeStruct((SEQ, 16, 128), F32...]
where the time goes in v6:
time: 147 us
  Pallas kernels  145 us (99%)
  local copies, waits for them, and re-layouts  1.87 us (1%)
    pallas_call x1, Pallas kernels, local(): pl.pallas_call(kernel, out_shape=jax.ShapeDtypeStruct((SEQ, 16, 128), F32...  145 us

profile of v6, /device:TPU:1, one launch (start us, length us, event | category | flops | bytes accessed | tf_op | source)
XLA Modules:
  0.0 147.0 jit_solution(11433112361824464164)
XLA Ops:
  0.0 145.2 %propagate.1 = f32[64,16,128]{2,1,0:T(8,128)} custom-call(s32[4]{0:T(128)} %lit.1, f32[2,4]{1,0:T(2,128)} %disp.1, f32[2,4]{1,0:T(2,128)} %nonlin.1, s32[4,64]{1,0:T(4,128)} %fibre_hbm.1, s32[4,64]{1,0:T(4,128)} %slot_hbm.1, f32[64,16,128]{2,1,0:T(8,128)} %bitcast.11, bf16[10,256,256]{2,1,0:T(8,128)(2,1)} %constant.4.clone.wide_hbm, ...), custom_call_target="tpu_custom_call" | custom-call | tf_op jit(solution)/shard_map/propagate/pallas_call | solution.py:578
  145.2 1.9 %copy.12 = f32[4,8,2,2,1024]{4,3,2,1,0:T(2,128)} copy(f32[4,8,2,2,1024]{4,3,2,1,0:T(2,128)} %bitcast.10) | data formatting | bytes 1048576

commit v7 on v5

--- a/solution.py
+++ b/solution.py
@@ -479,15 +479,13 @@
 
     lax.fori_loop(WAVE, 2 * WAVE, gather, 0)
     pl.semaphore_wait(column.at[1], 5)
-    for k in (8, 9, 10, 11, 12, 13):
+    for k in (14, 12, 10, 8, 15, 13, 11, 9):
         item_copy(k).start()
     lax.fori_loop(0, WAVE, gather, 0)
     for k in (1, 2, 3, 4, 5, 6, 7):
         item_copy(k).start()
     recv_items[0:2] = send_items[0:2]
     finish_near(1)
-    for k in (14, 15):
-        item_copy(k).start()
     finish_far(1, False)
     for k in range(1, 16):
         item_copy(k).wait_recv()
@@ -512,6 +510,23 @@
     finish_far(2, True)
     run_step(3, False)
     finish_near(3)
+
+    def drain_halo(f, carry):
+        for e in range(4):
+            halo_copy(e, 0, f).wait_send()
+            halo_copy(e, 1, f).wait_send()
+        return carry
+
+    lax.fori_loop(0, FIB, drain_halo, 0)
+    for e in range(3):
+        for k in range(1, 8):
+            near_copy(e, k).wait_send()
+        far_copy(e).wait_send()
+    for e in (0, 2):
+        side_copy(e, 0).wait_send()
+        side_copy(e, 1).wait_send()
+    for k in range(1, 16):
+        item_copy(k).wait_send()
     finish_far(3, False)
 
     def store(f):
@@ -530,22 +545,9 @@
 
     lax.fori_loop(0, FIB, last, 0)
 
-    def drain_halo(f, carry):
-        for e in range(4):
-            halo_copy(e, 0, f).wait_send()
-            halo_copy(e, 1, f).wait_send()
-        return carry
-
-    lax.fori_loop(0, FIB, drain_halo, 0)
-    for e in range(4):
-        for k in range(1, 8):
-            near_copy(e, k).wait_send()
-        far_copy(e).wait_send()
-    for e in (0, 2):
-        side_copy(e, 0).wait_send()
-        side_copy(e, 1).wait_send()
-    for k in range(1, 16):
-        item_copy(k).wait_send()
+    for k in range(1, 8):
+        near_copy(3, k).wait_send()
+    far_copy(3).wait_send()
     for f in range(FIB):
         store(f).wait()
 

time: 146 us -> 146 us (level)
  no operation moved by 1% of the time
where the time goes in v7:
time: 146 us; the launch traced here: 144 us
  Pallas kernels  142 us (97%)
  local copies, waits for them, and re-layouts  1.87 us (1%)
    pallas_call x1, Pallas kernels, local(): pl.pallas_call(kernel, out_shape=jax.ShapeDtypeStruct((SEQ, 16, 128), F32...  142 us

profile of v7, /device:TPU:1, one launch (start us, length us, event | category | flops | bytes accessed | tf_op | source)
XLA Modules:
  0.0 143.7 jit_solution(17367419463733082054)
XLA Ops:
  0.0 141.8 %propagate.1 = f32[64,16,128]{2,1,0:T(8,128)} custom-call(s32[4]{0:T(128)} %lit.1, f32[2,4]{1,0:T(2,128)} %disp.1, f32[2,4]{1,0:T(2,128)} %nonlin.1, s32[4,64]{1,0:T(4,128)} %fibre_hbm.1, s32[4,64]{1,0:T(4,128)} %slot_hbm.1, f32[64,16,128]{2,1,0:T(8,128)} %bitcast.11, bf16[10,256,256]{2,1,0:T(8,128)(2,1)} %constant.4.clone.wide_hbm, ...), custom_call_target="tpu_custom_call" | custom-call | tf_op jit(solution)/shard_map/propagate/pallas_call | solution.py:561
  141.8 1.9 %copy.12 = f32[4,8,2,2,1024]{4,3,2,1,0:T(2,128)} copy(f32[4,8,2,2,1024]{4,3,2,1,0:T(2,128)} %bitcast.10) | data formatting | bytes 1048576
